TPU v7x, 32 devices: a whole 2x2x4 slice. The times are simulated.
32 devices in a mesh: dp: 8 (over z, y), seq: 4 (over x, core).
Axes of the slice: x: 2, y: 2, z: 4, core: 2. Of those that a mesh axis runs over, the one named last changes fastest.
Arguments:
- tokens: bfloat16 [64, 320, 1024], P('dp', 'seq'), may hold values from -6 to 6
- keep: int32 [64, 320], P('dp'), may hold values from 0 to 1, as said below
- adapter_id: int32 [64], P('dp'), may hold values from 0 to 7
- w_qkv: bfloat16 [1024, 3072], P('dp'), may hold values from -0.1875 to 0.1875
- w_o: bfloat16 [1024, 1024], P('dp'), may hold values from -0.75 to 0.75
- w_up: bfloat16 [1024, 4096], P('dp'), may hold values from -0.1875 to 0.1875
- w_down: bfloat16 [4096, 1024], P('dp'), may hold values from -0.09375 to 0.09375
- ln1_gain: float32 [1024], replicated, may hold values from 0.1 to 1.9
- ln2_gain: float32 [1024], replicated, may hold values from 0.1 to 1.9
- qkv_in: bfloat16 [3, 8, 1024, 16], replicated, may hold values from -0.1875 to 0.1875
- qkv_out: bfloat16 [3, 8, 16, 1024], replicated, may hold values from -0.75 to 0.75
- o_in: bfloat16 [8, 1024, 16], replicated, may hold values from -0.1875 to 0.1875
- o_out: bfloat16 [8, 16, 1024], replicated, may hold values from -1.5 to 1.5
- up_in: bfloat16 [8, 1024, 16], replicated, may hold values from -0.1875 to 0.1875
- up_out: bfloat16 [8, 16, 4096], replicated, may hold values from -0.75 to 0.75
- down_in: bfloat16 [8, 4096, 16], replicated, may hold values from -0.09375 to 0.09375
- down_out: bfloat16 [8, 16, 1024], replicated, may hold values from -0.75 to 0.75
- cotangent: bfloat16 [64, 320, 1024], P('dp', 'seq'), may hold values from -6 to 6
Outputs:
- layer_out: bfloat16 [64, 320, 1024], P('dp', 'seq')
- grad_tokens: bfloat16 [64, 320, 1024], P('dp', 'seq')
- grad_qkv_in: float32 [3, 8, 1024, 16], replicated
- grad_qkv_out: float32 [3, 8, 16, 1024], replicated
- grad_o_in: float32 [8, 1024, 16], replicated
- grad_o_out: float32 [8, 16, 1024], replicated
- grad_up_in: float32 [8, 1024, 16], replicated
- grad_up_out: float32 [8, 16, 4096], replicated
- grad_down_in: float32 [8, 4096, 16], replicated
- grad_down_out: float32 [8, 16, 1024], replicated
Inputs may be any that keep to these rules, and one draw needn't show every extreme that they name: `keep`: each image keeps from 40 to all 320 of its tokens, at positions spread at random.
All inputs are finite; a program needn't handle non-finite values.
Results may differ from a plain program's by a relative error of at most 0.017.
The roundings to bfloat16 on the way count: a program that leaves them out, or rounds other values in their place, can miss the bound.
Values may be sent and summed in bfloat16 or wider, within the bound.
A program may use at most 192 MiB of HBM per device.

v0:
```python
from functools import partial

import jax
import jax.numpy as jnp
from jax import lax
from jax.sharding import PartitionSpec as P

HEAD_DIM = 64


def normalize(values, gains):
    row_mean = jnp.mean(values, -1, keepdims=True)
    centred = values - row_mean
    spread = jnp.mean(centred * centred, -1, keepdims=True)
    return centred * lax.rsqrt(spread + 1e-06) * gains


def adapted(inputs, weight, first_rank, second_rank):
    main = jnp.einsum("gld,de->gle", inputs, weight, preferred_element_type=jnp.float32)
    reduced = jnp.einsum(
        "gld,gdr->glr", inputs, first_rank, preferred_element_type=jnp.float32
    ).astype(jnp.bfloat16)
    return (
        main + jnp.einsum("glr,gre->gle", reduced, second_rank, preferred_element_type=jnp.float32),
        reduced,
    )


def adapted_back(inputs, weight, first_rank, second_rank, reduced, upstream):
    grad_reduced = jnp.einsum(
        "gle,gre->glr", upstream, second_rank, preferred_element_type=jnp.float32
    ).astype(jnp.bfloat16)
    grad_second = jnp.einsum("glr,gle->gre", reduced, upstream, preferred_element_type=jnp.float32)
    grad_first = jnp.einsum(
        "gld,glr->gdr", inputs, grad_reduced, preferred_element_type=jnp.float32
    )
    grad_inputs = jnp.einsum("gle,de->gld", upstream, weight, preferred_element_type=jnp.float32)
    grad_inputs = grad_inputs + jnp.einsum(
        "glr,gdr->gld", grad_reduced, first_rank, preferred_element_type=jnp.float32
    )
    return (grad_inputs, grad_first, grad_second)


def split_heads(values):
    groups, seq_len, local_width = values.shape
    return values.reshape(groups, seq_len, local_width // HEAD_DIM, HEAD_DIM)


def masked_scores(head_q, head_k, key_keep):
    score_scale = float(HEAD_DIM) ** (-0.5)
    scores = (
        jnp.einsum("gqhc,gkhc->ghqk", head_q, head_k, preferred_element_type=jnp.float32)
        * score_scale
    )
    return jnp.where(key_keep[:, None, None, :] > 0.5, scores, -1e30)


def attend(head_q, head_k, head_v, key_keep):
    groups, seq_len, local_width = head_q.shape
    scores = masked_scores(split_heads(head_q), split_heads(head_k), key_keep)
    row_max = jnp.max(scores, -1, keepdims=True)
    exponent = jnp.exp(scores - row_max)
    row_total = jnp.sum(exponent, -1, keepdims=True)
    attn_probs = (exponent / row_total).astype(jnp.bfloat16)
    mixed = jnp.einsum(
        "ghqk,gkhc->gqhc", attn_probs, split_heads(head_v), preferred_element_type=jnp.float32
    )
    return (
        mixed.astype(jnp.bfloat16).reshape(groups, seq_len, local_width),
        row_max + jnp.log(row_total),
    )


def attend_back(head_q, head_k, head_v, key_keep, log_total, grad_heads):
    groups, seq_len, local_width = head_q.shape
    score_scale = float(HEAD_DIM) ** (-0.5)
    query_split = split_heads(head_q)
    key_split = split_heads(head_k)
    grad_split = split_heads(grad_heads)
    attn_p = jnp.exp(masked_scores(query_split, key_split, key_keep) - log_total)
    grad_probs = jnp.einsum(
        "gqhc,gkhc->ghqk", grad_split, split_heads(head_v), preferred_element_type=jnp.float32
    )
    row_delta = jnp.sum(attn_p * grad_probs, -1, keepdims=True)
    grad_scores = (attn_p * (grad_probs - row_delta)).astype(jnp.bfloat16)
    grad_q = (
        jnp.einsum("ghqk,gkhc->gqhc", grad_scores, key_split, preferred_element_type=jnp.float32)
        * score_scale
    )
    grad_k = (
        jnp.einsum("ghqk,gqhc->gkhc", grad_scores, query_split, preferred_element_type=jnp.float32)
        * score_scale
    )
    grad_v = jnp.einsum(
        "ghqk,gqhc->gkhc",
        attn_p.astype(jnp.bfloat16),
        grad_split,
        preferred_element_type=jnp.float32,
    )
    shape_out = (groups, seq_len, local_width)
    return (
        grad_q.astype(jnp.bfloat16).reshape(shape_out),
        grad_k.astype(jnp.bfloat16).reshape(shape_out),
        grad_v.astype(jnp.bfloat16).reshape(shape_out),
    )


def fold_table(one_hot, per_image):
    return jnp.einsum("gi,gdr->idr", one_hot, per_image)


def per_device(
    tokens,
    keep,
    adapter_id,
    w_qkv,
    w_o,
    w_up,
    w_down,
    ln1_gain,
    ln2_gain,
    qkv_in,
    qkv_out,
    o_in,
    o_out,
    up_in,
    up_out,
    down_in,
    down_out,
    cotangent,
):
    frozen = (
        lax.all_gather(w_qkv, "dp", axis=0, tiled=True),
        lax.all_gather(w_o, "dp", axis=0, tiled=True),
        lax.all_gather(w_up, "dp", axis=0, tiled=True),
        lax.all_gather(w_down, "dp", axis=0, tiled=True),
    )
    full_qkv, full_o, full_up, full_down = frozen
    groups, local_len, model_width = tokens.shape
    offset = lax.axis_index("seq") * local_len
    keep_all = keep.astype(jnp.float32)
    keep_local = lax.dynamic_slice_in_dim(keep_all, offset, local_len, 1)[:, :, None]
    sel_qkv_in = jnp.take(qkv_in, adapter_id, axis=1)
    sel_qkv_out = jnp.take(qkv_out, adapter_id, axis=1)
    sel_o_in = jnp.take(o_in, adapter_id, axis=0)
    sel_o_out = jnp.take(o_out, adapter_id, axis=0)
    sel_up_in = jnp.take(up_in, adapter_id, axis=0)
    sel_up_out = jnp.take(up_out, adapter_id, axis=0)
    sel_down_in = jnp.take(down_in, adapter_id, axis=0)
    sel_down_out = jnp.take(down_out, adapter_id, axis=0)
    tokens_f = tokens.astype(jnp.float32)
    normed = normalize(tokens_f, ln1_gain).astype(jnp.bfloat16)
    projected = []
    reduced_qkv = []
    for column in range(3):
        block_cols = full_qkv[:, column * model_width : (column + 1) * model_width]
        projection, reduced = adapted(normed, block_cols, sel_qkv_in[column], sel_qkv_out[column])
        projected.append(projection.astype(jnp.bfloat16))
        reduced_qkv.append(reduced)
    head_q, head_k, head_v = (
        lax.all_to_all(projected[0], "seq", split_axis=2, concat_axis=1, tiled=True),
        lax.all_to_all(projected[1], "seq", split_axis=2, concat_axis=1, tiled=True),
        lax.all_to_all(projected[2], "seq", split_axis=2, concat_axis=1, tiled=True),
    )
    mixed_heads, log_total = attend(head_q, head_k, head_v, keep_all)
    mixed = lax.all_to_all(mixed_heads, "seq", split_axis=1, concat_axis=2, tiled=True)
    proj_o, reduced_o = adapted(mixed, full_o, sel_o_in, sel_o_out)
    after_attn = tokens_f + proj_o
    normed_two = normalize(after_attn, ln2_gain).astype(jnp.bfloat16)
    pre_act, reduced_up = adapted(normed_two, full_up, sel_up_in, sel_up_out)
    activated = jax.nn.gelu(pre_act, approximate=False).astype(jnp.bfloat16)
    proj_down, reduced_down = adapted(activated, full_down, sel_down_in, sel_down_out)
    layer_out = ((after_attn + proj_down) * keep_local).astype(jnp.bfloat16)
    back_weights = (
        lax.all_gather(w_qkv, "dp", axis=0, tiled=True),
        lax.all_gather(w_o, "dp", axis=0, tiled=True),
        lax.all_gather(w_up, "dp", axis=0, tiled=True),
        lax.all_gather(w_down, "dp", axis=0, tiled=True),
    )
    back_qkv, back_o, back_up, back_down = back_weights
    one_hot = (adapter_id[:, None] == jnp.arange(qkv_in.shape[1], dtype=jnp.int32)[None, :]).astype(
        jnp.float32
    )
    grad_layer = cotangent.astype(jnp.float32) * keep_local
    grad_down = grad_layer.astype(jnp.bfloat16)
    grad_activated, down_first, down_second = adapted_back(
        activated, back_down, sel_down_in, sel_down_out, reduced_down, grad_down
    )
    gelu_value, gelu_pull = jax.vjp(partial(jax.nn.gelu, approximate=False), pre_act)
    grad_pre = gelu_pull(grad_activated)[0].astype(jnp.bfloat16)
    grad_normed_two, up_first, up_second = adapted_back(
        normed_two, back_up, sel_up_in, sel_up_out, reduced_up, grad_pre
    )
    mlp_tables = (
        fold_table(one_hot, up_first),
        fold_table(one_hot, up_second),
        fold_table(one_hot, down_first),
        fold_table(one_hot, down_second),
    )
    norm_value, norm_two_pull = jax.vjp(partial(normalize, gains=ln2_gain), after_attn)
    grad_attn = grad_layer + norm_two_pull(grad_normed_two)[0]
    grad_proj = grad_attn.astype(jnp.bfloat16)
    grad_mixed, o_first, o_second = adapted_back(
        mixed, back_o, sel_o_in, sel_o_out, reduced_o, grad_proj
    )
    out_tables = (fold_table(one_hot, o_first), fold_table(one_hot, o_second))
    grad_heads = lax.all_to_all(
        grad_mixed.astype(jnp.bfloat16), "seq", split_axis=2, concat_axis=1, tiled=True
    )
    grad_hq, grad_hk, grad_hv = attend_back(head_q, head_k, head_v, keep_all, log_total, grad_heads)
    grad_proj_q, grad_proj_k, grad_proj_v = (
        lax.all_to_all(grad_hq, "seq", split_axis=1, concat_axis=2, tiled=True),
        lax.all_to_all(grad_hk, "seq", split_axis=1, concat_axis=2, tiled=True),
        lax.all_to_all(grad_hv, "seq", split_axis=1, concat_axis=2, tiled=True),
    )
    grad_projected = (grad_proj_q, grad_proj_k, grad_proj_v)
    grad_normed = jnp.zeros(tokens.shape, jnp.float32)
    qkv_first = []
    qkv_second = []
    for column in range(3):
        block_cols = back_qkv[:, column * model_width : (column + 1) * model_width]
        grad_part, first_part, second_part = adapted_back(
            normed,
            block_cols,
            sel_qkv_in[column],
            sel_qkv_out[column],
            reduced_qkv[column],
            grad_projected[column],
        )
        grad_normed = grad_normed + grad_part
        qkv_first.append(fold_table(one_hot, first_part))
        qkv_second.append(fold_table(one_hot, second_part))
    norm_one_value, norm_one_pull = jax.vjp(partial(normalize, gains=ln1_gain), tokens_f)
    grad_input = (grad_attn + norm_one_pull(grad_normed)[0]).astype(jnp.bfloat16)
    qkv_tables = (jnp.stack(qkv_first, 0), jnp.stack(qkv_second, 0))
    summed = lax.psum(
        (
            qkv_tables[0],
            qkv_tables[1],
            out_tables[0],
            out_tables[1],
            mlp_tables[0],
            mlp_tables[1],
            mlp_tables[2],
            mlp_tables[3],
        ),
        ("dp", "seq"),
    )
    return (
        layer_out,
        grad_input,
        summed[0],
        summed[1],
        summed[2],
        summed[3],
        summed[4],
        summed[5],
        summed[6],
        summed[7],
    )


def solution(mesh):
    return jax.shard_map(
        per_device,
        mesh=mesh,
        in_specs=(
            P("dp", "seq", None),
            P("dp", None),
            P("dp"),
            P("dp", None),
            P("dp", None),
            P("dp", None),
            P("dp", None),
            P(),
            P(),
            P(),
            P(),
            P(),
            P(),
            P(),
            P(),
            P(),
            P(),
            P("dp", "seq", None),
        ),
        out_specs=(
            P("dp", "seq", None),
            P("dp", "seq", None),
            P(),
            P(),
            P(),
            P(),
            P(),
            P(),
            P(),
            P(),
        ),
        check_vma=False,
    )
```

profile of v0, /device:TPU:31, one launch (start us, length us, event | category | flops | bytes accessed | tf_op | source)
XLA Modules:
  0.0 816.0 jit_solution(7629603083224695751)
XLA Ops:
  18.6 88.5 %all-gather.5.cloned.1.call-done = bf16[1024,3072]{1,0:T(8,128)(2,1)} async-done(((bf16[128,3072]{1,0:T(8,128)(2,1)}), bf16[1024,3072]{1,0:T(8,128)(2,1)}) %all-gather.5.cloned.1.call-update) | async-done | bytes 6291472 | tf_op jit(solution)/shard_map/all_gather | solution.py:133
  111.9 3.9 copy.76
  115.8 5.2 all-to-all-start
  127.4 3.9 copy.78
  131.4 13.6 %all-to-all-done = bf16[8,80,1024]{1,0,2:T(8,128)(2,1)} async-done(((bf16[8,80,1024]{1,0,2:T(8,128)(2,1)}), bf16[8,80,1024]{1,0,2:T(8,128)(2,1)}, u32[]{:S(2)}, u32[]{:S(2)}) %all-to-all-start) | async-done | bytes 1310752 | tf_op jit(solution)/shard_map/all_to_all | solution.py:163
  145.0 6.3 all-to-all-start.1
  157.6 4.0 copy.80
  161.6 13.6 %all-to-all-done.1 = bf16[8,80,1024]{1,0,2:T(8,128)(2,1)} async-done(((bf16[8,80,1024]{1,0,2:T(8,128)(2,1)}), bf16[8,80,1024]{1,0,2:T(8,128)(2,1)}, u32[]{:S(2)}, u32[]{:S(2)}) %all-to-all-start.1) | async-done | bytes 1310752 | tf_op jit(solution)/shard_map/all_to_all | solution.py:161
  175.2 6.3 all-to-all-start.2
  182.1 4.5 copy.165
  186.6 4.3 reshape.131
  190.9 4.5 copy.164
  195.5 4.3 reshape.132
  199.8 5.6 all-to-all-done.2
  205.4 4.5 copy.163
  209.9 4.6 reshape.133
  214.5 10.8 %fusion.126 = (f32[8,4,320]{2,1,0:T(4,128)S(1)}, f32[8,4,320,320]{2,3,1,0:T(8,128)}) fusion(bf16[8,320,4,64]{1,3,2,0:T(8,128)(2,1)} %reshape.132, bf16[8,320,4,64]{1,3,2,0:T(8,128)(2,1)} %reshape.133, pred[8,320]{1,0:T(8,128)(4,1)S(1)} %broadcast_compare_fusion), kind=kOutput, calls=%fused_computation.204 | convolution fusion | flops 429250560 | bytes 15772160 | tf_op jit(solution)/shard_map/gqhc,gkhc->ghqk/dot_general | solution.py:52
  225.4 8.3 %fusion = f32[8,4,320]{2,1,0:T(4,128)S(1)} fusion(f32[8,4,320,320]{2,3,1,0:T(8,128)} %get-tuple-element.57, f32[8,4,320]{2,1,0:T(4,128)S(1)} %get-tuple-element.56), kind=kLoop, calls=%fused_computation.15 | loop fusion | flops 6543360 | bytes 13189120 | tf_op jit(solution)/shard_map/reduce_sum | solution.py:63
  233.7 9.7 %fusion.39 = bf16[8,4,64,320]{3,2,1,0:T(8,128)(2,1)} fusion(bf16[8,320,4,64]{1,3,2,0:T(8,128)(2,1)S(1)} %copy-done.27, f32[8,4,320,320]{2,3,1,0:T(8,128)} %get-tuple-element.57, f32[8,4,320]{2,1,0:T(4,128)S(1)} %fusion, f32[8,4,320]{2,1,0:T(4,128)S(1)} %get-tuple-element.56), kind=kOutput, calls=%fused_computation.95 | convolution fusion | flops 429916160 | bytes 15810560 | tf_op jit(solution)/shard_map/ghqk,gkhc->gqhc/dot_general | solution.py:65
  246.2 6.4 all-to-all-start.3
  263.2 4.8 all-to-all-done.3
  271.5 3.7 all_to_all.108
  284.4 8.5 %fusion.14 = f32[8,80,4096]{2,1,0:T(8,128)S(1)} fusion(bf16[8,80,1024]{2,1,0:T(8,128)(2,1)} %copy-done.30, bf16[1024,4096]{1,0:T(8,128)(2,1)} %all-gather.9.cloned.1.call-done), kind=kOutput, calls=%fused_computation.43 | convolution fusion | flops 5368709120 | bytes 20185088 | tf_op jit(solution)/shard_map/gld,de->gle/dot_general | solution.py:19
  292.9 6.2 fusion.30
  299.1 4.0 copy-done.24
  303.0 24.6 %multiply_convert_fusion.1 = (bf16[8,80,4096]{2,1,0:T(8,128)(2,1)}, f32[8,80,4096]{2,1,0:T(8,128)}) fusion(f32[8,80,4096]{2,1,0:T(8,128)S(1)} %get-tuple-element.60, u8[80,4096]{1,0:T(8,128)(4,1)S(1)} %get-tuple-element.43, u8[80,4096]{1,0:T(8,128)(4,1)S(1)} %get-tuple-element.42), kind=kLoop, calls=%fused_computation.24 | loop fusion | flops 183500800 | bytes 26869760 | tf_op jit(solution)/shard_map/convert_element_type | solution.py:171
  327.6 78.7 %all-gather.11.cloned.1.call-done = bf16[4096,1024]{1,0:T(8,128)(2,1)} async-done(((bf16[512,1024]{1,0:T(8,128)(2,1)}), bf16[4096,1024]{1,0:T(8,128)(2,1)}) %all-gather.11.cloned.1.call-update) | async-done | bytes 8388624 | tf_op jit(solution)/shard_map/all_gather | solution.py:136
  406.3 11.3 %fusion.8 = f32[8,80,4096]{2,1,0:T(8,128)} fusion(bf16[4096,1024]{1,0:T(8,128)(2,1)} %all-gather.11.cloned.1.call-done, bf16[8,80,1024]{2,1,0:T(8,128)(2,1)} %param.39, f32[8,80]{1,0:T(8,128)S(1)} %constant_dynamic-slice_fusion), kind=kOutput, calls=%fused_computation.37 | convolution fusion | flops 5370675200 | bytes 20187648 | tf_op jit(solution)/shard_map/gle,de->gld/dot_general | solution.py:37
  417.6 12.8 %add_convert_fusion = bf16[8,80,4096]{2,1,0:T(8,128)(2,1)S(1)} fusion(f32[8,80,4096]{2,1,0:T(8,128)} %get-tuple-element.55, f32[8,80,4096]{2,1,0:T(8,128)} %fusion.8, f32[8,80,4096]{2,1,0:T(8,128)} %copy-done.24, bf16[8,80,16]{1,2,0:T(8,128)(2,1)S(1)} %convolution_convert_fusion.4, bf16[8,4096,16]{1,2,0:T(8,128)(2,1)S(1)} %gather_fusion.3, ...), kind=kOutput, calls=%fused_computation.23 | convolution fusion | flops 123731968 | bytes 37769224 | tf_op jit(solution)/shard_map/glr,gdr->gld/dot_general | solution.py:38
  432.0 8.4 %fusion.12 = f32[8,80,1024]{2,1,0:T(8,128)S(1)} fusion(bf16[8,80,4096]{2,1,0:T(8,128)(2,1)S(1)} %add_convert_fusion, bf16[1024,4096]{1,0:T(8,128)(2,1)} %all-gather.9.cloned.1.call-done), kind=kOutput, calls=%fused_computation.41 | convolution fusion | flops 5368709120 | bytes 16252928 | tf_op jit(solution)/shard_map/gle,de->gld/dot_general | solution.py:37
  452.9 3.9 copy.86
  456.9 5.5 all-to-all-start.4
  473.1 13.1 %all-to-all-done.4 = bf16[8,80,1024]{1,0,2:T(8,128)(2,1)} async-done(((bf16[8,80,1024]{1,0,2:T(8,128)(2,1)}), bf16[8,80,1024]{1,0,2:T(8,128)(2,1)}, u32[]{:S(2)}, u32[]{:S(2)}) %all-to-all-start.4) | async-done | bytes 1310752 | tf_op jit(solution)/shard_map/all_to_all | solution.py:207
  486.3 4.5 copy.162
  490.8 4.3 reshape.135
  495.1 9.8 %fusion.40 = bf16[8,4,64,320]{3,2,1,0:T(8,128)(2,1)} fusion(bf16[8,320,4,64]{1,3,2,0:T(8,128)(2,1)} %reshape.135, f32[8,4,320,320]{2,3,1,0:T(8,128)} %get-tuple-element.57, f32[8,4,320]{2,1,0:T(4,128)S(1)} %bitcast.202), kind=kOutput, calls=%fused_computation.96 | convolution fusion | flops 426639360 | bytes 15769600 | tf_op jit(solution)/shard_map/ghqk,gqhc->gkhc/dot_general | solution.py:94
  504.9 10.3 %multiply_reduce_fusion = (f32[8,4,320]{2,1,0:T(4,128)S(1)}, f32[8,4,320,320]{2,3,1,0:T(8,128)}) fusion(f32[8,4,320,320]{2,3,1,0:T(8,128)} %get-tuple-element.57, f32[8,4,320]{2,1,0:T(4,128)S(1)} %bitcast.203, bf16[8,320,4,64]{1,3,2,0:T(8,128)(2,1)S(1)} %copy-done.16, bf16[8,320,4,64]{1,3,2,0:T(8,128)(2,1)S(1)} %copy-done.28), kind=kOutput, calls=%fused_computation.9 | convolution fusion | flops 429250560 | bytes 28917760 | tf_op jit(solution)/shard_map/gqhc,gkhc->ghqk/dot_general | solution.py:81
  518.0 6.4 all-to-all-start.7
  524.4 11.2 %multiply_convert_fusion = bf16[8,4,320,320]{2,3,1,0:T(8,128)(2,1)S(1)} fusion(f32[8,4,320,320]{2,3,1,0:T(8,128)} %get-tuple-element.64, f32[8,4,320,320]{2,3,1,0:T(8,128)} %get-tuple-element.57, f32[8,4,320]{2,1,0:T(4,128)S(1)} %get-tuple-element.63, f32[8,4,320]{2,1,0:T(4,128)S(1)} %bitcast.204), kind=kLoop, calls=%fused_computation.8 | loop fusion | flops 13107200 | bytes 32849920 | tf_op jit(solution)/shard_map/convert_element_type | solution.py:85
  535.6 3.7 multiply_convert_fusion.2
  542.1 4.3 all-to-all-start.6
  550.0 5.9 multiply_convert_fusion.3
  562.1 3.6 all_to_all.123
  565.8 4.3 all-to-all-start.5
  573.6 4.1 all_to_all.119
  589.0 3.7 all_to_all.115
  602.0 9.8 %fusion.10 = f32[8,80,1024]{2,1,0:T(8,128)S(1)} fusion(bf16[8,80,4096]{2,1,0:T(8,128)(2,1)} %get-tuple-element.54, bf16[4096,1024]{1,0:T(8,128)(2,1)} %all-gather.11.cloned.1.call-done), kind=kOutput, calls=%fused_computation.39 | convolution fusion | flops 5368709120 | bytes 16252928 | tf_op jit(solution)/shard_map/gld,de->gle/dot_general | solution.py:19
  627.7 166.3 %all-reduce.3.cloned.1.call-done = (f32[3,8,1024,16]{2,1,3,0:T(8,128)}, f32[3,8,16,1024]{3,1,2,0:T(8,128)}, f32[8,1024,16]{1,0,2:T(8,128)}, f32[8,16,1024]{2,0,1...) async-done(((f32[3,8,1024,16]{2,1,3,0:T(8,128)}, f32[3,8,16,1024]{3,1,2,0:T(8,128)}, ...) | async-done | bytes 9437200 | tf_op jit(solution)/shard_map/psum | solution.py:236
  (291 shorter events, 150.1 us)
Async XLA Ops:
  7.2 250.3 %copy-start = (bf16[8,16,4096]{2,1,0:T(8,128)(2,1)S(1)}, bf16[8,16,4096]{2,1,0:T(8,128)(2,1)}, u32[]{:S(2)}) copy-start(bf16[8,16,4096]{2,1,0:T(8,128)(2,1)} %param.36) | copy-start | bytes 3145732
  7.2 99.9 %all-gather.5.cloned.1.call-start = ((), (), s32[]{:S(2)}) async-start(), calls=%async_computation.8 | async-start | bytes 7077888 | tf_op jit(solution)/shard_map/all_gather | solution.py:133
  7.9 269.0 %all-gather.7.cloned.1.call-start = ((), (), s32[]{:S(2)}) async-start(), calls=%async_computation.9 | async-start | bytes 2359296 | tf_op jit(solution)/shard_map/all_gather | solution.py:134
  8.7 275.7 %all-gather.9.cloned.1.call-start = ((), (), s32[]{:S(2)}) async-start(), calls=%async_computation.10 | async-start | bytes 9437184 | tf_op jit(solution)/shard_map/all_gather | solution.py:135
  14.5 138.3 %copy-start.59 = (f32[8,80]{1,0:T(8,128)}, f32[8,80]{1,0:T(8,128)S(1)}, u32[]{:S(2)}) copy-start(f32[8,80]{1,0:T(8,128)S(1)} %broadcast_multiply_fusion.1) | copy-start | bytes 7684
  16.3 245.0 %copy-start.73 = (pred[8]{0:T(512)(128)(4,1)}, pred[8]{0:T(512)(128)(4,1)S(1)}, u32[]{:S(2)}) copy-start(pred[8]{0:T(512)(128)(4,1)S(1)} %compare_and_fusion) | copy-start | bytes 28
  16.9 135.9 %copy-start.69 = (f32[8,80]{1,0:T(8,128)}, f32[8,80]{1,0:T(8,128)S(1)}, u32[]{:S(2)}) copy-start(f32[8,80]{1,0:T(8,128)S(1)} %fusion.86) | copy-start | bytes 7684
  17.1 90.0 %copy-start.9 = (bf16[8,80,1024]{2,1,0:T(8,128)(2,1)S(1)}, bf16[8,80,1024]{2,1,0:T(8,128)(2,1)}, u32[]{:S(2)}) copy-start(bf16[8,80,1024]{2,1,0:T(8,128)(2,1)} %param.22) | copy-start | bytes 3932164
  18.0 138.0 %copy-start.25 = (bf16[3,8,16,1024]{3,2,1,0:T(8,128)(2,1)}, bf16[3,8,16,1024]{3,2,1,0:T(8,128)(2,1)S(1)}, u32[]{:S(2)}) copy-start(bf16[3,8,16,1024]{3,2,1,0:T(8,128)(2,1)S(1)} %fusion.55) | copy-start | bytes 2359300
  18.6 91.7 %copy-start.52 = (bf16[8,80,16]{1,2,0:T(8,128)(2,1)}, bf16[8,80,16]{1,2,0:T(8,128)(2,1)S(1)}, u32[]{:S(2)}) copy-start(bf16[8,80,16]{1,2,0:T(8,128)(2,1)S(1)} %convolution_convert_fusion.9) | copy-start | bytes 61444
  115.8 29.2 %all-to-all-start = ((bf16[8,80,1024]{1,0,2:T(8,128)(2,1)}), bf16[8,80,1024]{1,0,2:T(8,128)(2,1)}, u32[]{:S(2)}, u32[]{:S(2)}) async-start(bf16[8,80,1024]{1,0,2:T(8,128)(2,1)} %copy.76), calls=%async_computation | async-start | bytes 4194304 | tf_op jit(solution)/shard_map/all_to_all | solution.py:163
  145.0 30.2 %all-to-all-start.1 = ((bf16[8,80,1024]{1,0,2:T(8,128)(2,1)}), bf16[8,80,1024]{1,0,2:T(8,128)(2,1)}, u32[]{:S(2)}, u32[]{:S(2)}) async-start(bf16[8,80,1024]{1,0,2:T(8,128)(2,1)} %copy.78), calls=%async_computation.1 | async-start | bytes 4194304 | tf_op jit(solution)/shard_map/all_to_all | solution.py:161
  161.6 20.5 %copy-start.64 = (s32[8,320]{1,0:T(8,128)S(1)}, s32[8,320]{1,0:T(8,128)}, u32[]{:S(2)}) copy-start(s32[8,320]{1,0:T(8,128)} %param.23) | copy-start | bytes 30724
  175.2 30.2 %all-to-all-start.2 = ((bf16[8,80,1024]{1,0,2:T(8,128)(2,1)}), bf16[8,80,1024]{1,0,2:T(8,128)(2,1)}, u32[]{:S(2)}, u32[]{:S(2)}) async-start(bf16[8,80,1024]{1,0,2:T(8,128)(2,1)} %copy.80), calls=%async_computation.2 | async-start | bytes 4194304 | tf_op jit(solution)/shard_map/all_to_all | solution.py:162
  181.5 224.9 %all-gather.11.cloned.1.call-start = ((), (), s32[]{:S(2)}) async-start(), calls=%async_computation.11 | async-start | bytes 9437184 | tf_op jit(solution)/shard_map/all_gather | solution.py:136
  225.3 8.3 %copy-start.27 = (bf16[8,320,4,64]{1,3,2,0:T(8,128)(2,1)S(1)}, bf16[8,320,4,64]{1,3,2,0:T(8,128)(2,1)}, u32[]{:S(2)}) copy-start(bf16[8,320,4,64]{1,3,2,0:T(8,128)(2,1)} %reshape.131) | copy-start | bytes 3932164
  243.3 9.3 %copy-start.14 = (bf16[8,1024,16]{1,2,0:T(8,128)(2,1)S(1)}, bf16[8,1024,16]{1,2,0:T(8,128)(2,1)}, u32[]{:S(2)}) copy-start(bf16[8,1024,16]{1,2,0:T(8,128)(2,1)} %param.33) | copy-start | bytes 786436
  246.2 21.9 %all-to-all-start.3 = ((bf16[8,320,256]{2,0,1:T(8,128)(2,1)}), bf16[8,320,256]{2,0,1:T(8,128)(2,1)}, u32[]{:S(2)}, u32[]{:S(2)}) async-start(bf16[8,320,256]{2,0,1:T(8,128)(2,1)} %copy.83), calls=%async_computation.3 | async-start | bytes 2621440 | tf_op jit(solution)/shard_map/all_to_all | solution.py:166
  261.2 6.8 copy-start.39
  261.3 180.9 %copy-start.56 = (f32[8,80]{1,0:T(8,128)}, f32[8,80]{1,0:T(8,128)S(1)}, u32[]{:S(2)}) copy-start(f32[8,80]{1,0:T(8,128)S(1)} %constant_dynamic-slice_fusion) | copy-start | bytes 7684
  263.2 154.5 %copy-start.71 = (bf16[8,80,16]{1,2,0:T(8,128)(2,1)}, bf16[8,80,16]{1,2,0:T(8,128)(2,1)S(1)}, u32[]{:S(2)}) copy-start(bf16[8,80,16]{1,2,0:T(8,128)(2,1)S(1)} %convolution_convert_fusion.4) | copy-start | bytes 61444
  268.1 7.1 copy-start.12
  268.1 7.1 copy-start.74
  284.4 8.5 %copy-start.42 = (bf16[8,16,4096]{2,1,0:T(8,128)(2,1)S(1)}, bf16[8,16,4096]{2,1,0:T(8,128)(2,1)}, u32[]{:S(2)}) copy-start(bf16[8,16,4096]{2,1,0:T(8,128)(2,1)} %gather_fusion.2) | copy-start | bytes 3145732
  417.6 12.9 %copy-start.43 = (bf16[8,16,4096]{2,1,0:T(8,128)(2,1)S(1)}, bf16[8,16,4096]{2,1,0:T(8,128)(2,1)}, u32[]{:S(2)}) copy-start(bf16[8,16,4096]{2,1,0:T(8,128)(2,1)} %gather_fusion.2) | copy-start | bytes 3145732
  432.0 8.4 %copy-start.3 = (f32[8,80,1024]{2,1,0:T(8,128)S(1)}, f32[8,80,1024]{2,1,0:T(8,128)}, u32[]{:S(2)}) copy-start(f32[8,80,1024]{2,1,0:T(8,128)} %copy-done.2) | copy-start | bytes 7864324
  456.9 5.5 copy-start.62
  456.9 8.7 %copy-start.57 = (f32[8,80]{1,0:T(8,128)S(1)}, f32[8,80]{1,0:T(8,128)}, u32[]{:S(2)}) copy-start(f32[8,80]{1,0:T(8,128)} %copy-done.56) | copy-start | bytes 7684
  456.9 29.4 %all-to-all-start.4 = ((bf16[8,80,1024]{1,0,2:T(8,128)(2,1)}), bf16[8,80,1024]{1,0,2:T(8,128)(2,1)}, u32[]{:S(2)}, u32[]{:S(2)}) async-start(bf16[8,80,1024]{1,0,2:T(8,128)(2,1)} %copy.86), calls=%async_computation.4 | async-start | bytes 4194304 | tf_op jit(solution)/shard_map/all_to_all | solution.py:207
  495.1 9.8 %copy-start.16 = (bf16[8,320,4,64]{1,3,2,0:T(8,128)(2,1)S(1)}, bf16[8,320,4,64]{1,3,2,0:T(8,128)(2,1)}, u32[]{:S(2)}) copy-start(bf16[8,320,4,64]{1,3,2,0:T(8,128)(2,1)} %reshape.135) | copy-start | bytes 3932164
  495.1 9.8 %copy-start.28 = (bf16[8,320,4,64]{1,3,2,0:T(8,128)(2,1)S(1)}, bf16[8,320,4,64]{1,3,2,0:T(8,128)(2,1)}, u32[]{:S(2)}) copy-start(bf16[8,320,4,64]{1,3,2,0:T(8,128)(2,1)} %reshape.131) | copy-start | bytes 3932164
  518.0 24.1 %all-to-all-start.7 = ((bf16[8,320,256]{2,0,1:T(8,128)(2,1)}), bf16[8,320,256]{2,0,1:T(8,128)(2,1)}, u32[]{:S(2)}, u32[]{:S(2)}) async-start(bf16[8,320,256]{2,0,1:T(8,128)(2,1)} %copy.97), calls=%async_computation.7 | async-start | bytes 2621440 | tf_op jit(solution)/shard_map/all_to_all | solution.py:214
  524.4 11.2 %copy-start.17 = (bf16[8,320,4,64]{1,3,2,0:T(8,128)(2,1)S(1)}, bf16[8,320,4,64]{1,3,2,0:T(8,128)(2,1)}, u32[]{:S(2)}) copy-start(bf16[8,320,4,64]{1,3,2,0:T(8,128)(2,1)} %reshape.132) | copy-start | bytes 3932164
  542.1 23.7 %all-to-all-start.6 = ((bf16[8,320,256]{2,0,1:T(8,128)(2,1)}), bf16[8,320,256]{2,0,1:T(8,128)(2,1)}, u32[]{:S(2)}, u32[]{:S(2)}) async-start(bf16[8,320,256]{2,0,1:T(8,128)(2,1)} %copy.93), calls=%async_computation.6 | async-start | bytes 2621440 | tf_op jit(solution)/shard_map/all_to_all | solution.py:213
  565.8 19.8 %all-to-all-start.5 = ((bf16[8,320,256]{2,0,1:T(8,128)(2,1)}), bf16[8,320,256]{2,0,1:T(8,128)(2,1)}, u32[]{:S(2)}, u32[]{:S(2)}) async-start(bf16[8,320,256]{2,0,1:T(8,128)(2,1)} %copy.89), calls=%async_computation.5 | async-start | bytes 2621440 | tf_op jit(solution)/shard_map/all_to_all | solution.py:212
  570.1 223.9 %all-reduce.3.cloned.1.call-start = ((), (), s32[]{:S(2)}) async-start(), calls=%async_computation.12 | async-start | bytes 18874368 | tf_op jit(solution)/shard_map/psum | solution.py:236
  570.1 7.6 copy-start.26
  573.6 6.0 copy-start.53
  589.0 5.5 copy-start.51
  589.0 7.1 copy-start.60
  589.0 7.1 copy-start.70
  589.0 7.1 copy-start.78
  602.0 9.9 %copy-start.4 = (f32[8,80,1024]{2,1,0:T(8,128)S(1)}, f32[8,80,1024]{2,1,0:T(8,128)}, u32[]{:S(2)}) copy-start(f32[8,80,1024]{2,1,0:T(8,128)} %copy-done.2) | copy-start | bytes 7864324
  602.0 9.9 %copy-start.40 = (bf16[8,16,1024]{2,1,0:T(8,128)(2,1)S(1)}, bf16[8,16,1024]{2,1,0:T(8,128)(2,1)}, u32[]{:S(2)}) copy-start(bf16[8,16,1024]{2,1,0:T(8,128)(2,1)} %copy-done.39) | copy-start | bytes 786436
  602.0 9.9 %copy-start.58 = (f32[8,80]{1,0:T(8,128)S(1)}, f32[8,80]{1,0:T(8,128)}, u32[]{:S(2)}) copy-start(f32[8,80]{1,0:T(8,128)} %copy-done.56) | copy-start | bytes 7684
  602.0 9.9 %copy-start.75 = (pred[8]{0:T(512)(128)(4,1)S(1)}, pred[8]{0:T(512)(128)(4,1)}, u32[]{:S(2)}) copy-start(pred[8]{0:T(512)(128)(4,1)} %copy-done.73) | copy-start | bytes 28
  611.9 6.7 slice-start.2
  794.0 5.7 copy-start.48
  (50 other events, 145.6 us)
Sparse Core Ops, SparseCore 0:
  10.2 96.8 all-gather.4
  109.2 47.0 all-gather.6
  158.4 123.2 all-gather.8
  283.7 122.6 all-gather.10
  602.1 191.8 all-reduce.2
where the time goes:
time: 828 us; the launch traced here: 816 us
  waiting for transfers between devices  390 us (47%)
  matrix products  180 us (22%)
  local copies, waits for them, and re-layouts  129 us (16%)
  other arithmetic  56.4 us (7%)
  starting transfers between devices  45.4 us (5%)
  between operations  15.1 us (2%)
    psum x1, waiting for transfers between devices, per_device(): lax.psum((qkv_tables[0], qkv_tables[1], out_tables[0], out_tables[1], mlp...  166 us
    all_gather x1, waiting for transfers between devices, per_device(): lax.all_gather(w_qkv, 'dp', axis=0, tiled=True)  88.5 us
    all_gather x1, waiting for transfers between devices, per_device(): lax.all_gather(w_down, 'dp', axis=0, tiled=True)  78.7 us
    dot_general x6, matrix products, adapted(): jnp.einsum('gld,de->gle', inputs, weight, preferred_element_type=jnp.floa...  31.4 us
    dot_general x6, matrix products, adapted_back(): jnp.einsum('gle,de->gld', upstream, weight, preferred_element_type=jnp.fl...  27.7 us
    unnamed x178, local copies, waits for them, and re-layouts  27.2 us
    convert_element_type x1, other arithmetic, per_device(): activated = jax.nn.gelu(pre_act, approximate=False).astype(jnp.bfloat16)  24.6 us
    dot_general x6, matrix products, adapted_back(): jnp.einsum('glr,gdr->gld', grad_reduced, first_rank, preferred_element_ty...  17.8 us
  transfers between devices with their start and end apart: 13, of which 9 were waited for; matrix products, arithmetic and copies ran while one was open for 28% of the time, Pallas kernels for 0%

commit v1 on v0

v1 whole, which is shorter than its diff:
```python
from functools import partial

import jax
import jax.numpy as jnp
from jax import lax
from jax.experimental import pallas as pl
from jax.sharding import PartitionSpec as P

HEAD_DIM = 64
PAIR = 128


def normalize(values, gains):
    row_mean = jnp.mean(values, -1, keepdims=True)
    centred = values - row_mean
    spread = jnp.mean(centred * centred, -1, keepdims=True)
    return centred * lax.rsqrt(spread + 1e-06) * gains


def adapted(inputs, weight, first_rank, second_rank):
    main = jnp.einsum("gld,de->gle", inputs, weight, preferred_element_type=jnp.float32)
    reduced = jnp.einsum(
        "gld,gdr->glr", inputs, first_rank, preferred_element_type=jnp.float32
    ).astype(jnp.bfloat16)
    return (
        main + jnp.einsum("glr,gre->gle", reduced, second_rank, preferred_element_type=jnp.float32),
        reduced,
    )


def adapted_back(inputs, weight, first_rank, second_rank, reduced, upstream):
    grad_reduced = jnp.einsum(
        "gle,gre->glr", upstream, second_rank, preferred_element_type=jnp.float32
    ).astype(jnp.bfloat16)
    grad_second = jnp.einsum("glr,gle->gre", reduced, upstream, preferred_element_type=jnp.float32)
    grad_first = jnp.einsum(
        "gld,glr->gdr", inputs, grad_reduced, preferred_element_type=jnp.float32
    )
    grad_inputs = jnp.einsum("gle,de->gld", upstream, weight, preferred_element_type=jnp.float32)
    grad_inputs = grad_inputs + jnp.einsum(
        "glr,gdr->gld", grad_reduced, first_rank, preferred_element_type=jnp.float32
    )
    return (grad_inputs, grad_first, grad_second)


def head_masks(shape):
    lane = lax.broadcasted_iota(jnp.int32, shape, 1)
    return tuple((lane // HEAD_DIM) == half for half in range(PAIR // HEAD_DIM))


def matmul(left, right, left_dim, right_dim):
    return lax.dot_general(
        left, right, (((left_dim,), (right_dim,)), ((), ())), preferred_element_type=jnp.float32
    )


def probabilities(query, key, key_keep):
    scores = matmul(query, key, 1, 1) * (float(HEAD_DIM) ** (-0.5))
    scores = jnp.where(key_keep > 0.5, scores, -1e30)
    exponent = jnp.exp(scores - jnp.max(scores, -1, keepdims=True))
    return exponent / jnp.sum(exponent, -1, keepdims=True)


def attend_kernel(keep_ref, q_ref, k_ref, v_ref, out_ref):
    query, key, value = q_ref[0], k_ref[0], v_ref[0]
    masks = head_masks(query.shape)
    mixed = jnp.zeros(query.shape, jnp.float32)
    for mask in masks:
        probs = probabilities(jnp.where(mask, query, 0), key, keep_ref[0])
        mixed = jnp.where(mask, matmul(probs.astype(jnp.bfloat16), value, 1, 0), mixed)
    out_ref[0] = mixed.astype(jnp.bfloat16)


def attend_back_kernel(keep_ref, q_ref, k_ref, v_ref, g_ref, dq_ref, dk_ref, dv_ref):
    query, key, value, grad = q_ref[0], k_ref[0], v_ref[0], g_ref[0]
    scale = float(HEAD_DIM) ** (-0.5)
    masks = head_masks(query.shape)
    grad_q = jnp.zeros(query.shape, jnp.float32)
    grad_k, grad_v = grad_q, grad_q
    for mask in masks:
        probs = probabilities(jnp.where(mask, query, 0), key, keep_ref[0])
        grad_probs = matmul(jnp.where(mask, grad, 0), value, 1, 1)
        row_delta = jnp.sum(probs * grad_probs, -1, keepdims=True)
        grad_scores = (probs * (grad_probs - row_delta)).astype(jnp.bfloat16)
        grad_q = jnp.where(mask, matmul(grad_scores, key, 1, 0), grad_q)
        grad_k = jnp.where(mask, matmul(grad_scores, query, 0, 0), grad_k)
        grad_v = jnp.where(mask, matmul(probs.astype(jnp.bfloat16), grad, 0, 0), grad_v)
    dq_ref[0] = (grad_q * scale).astype(jnp.bfloat16)
    dk_ref[0] = (grad_k * scale).astype(jnp.bfloat16)
    dv_ref[0] = grad_v.astype(jnp.bfloat16)


def attention_call(kernel, key_keep, arrays, outputs):
    groups, seq_len, width = arrays[0].shape
    block = pl.BlockSpec((1, seq_len, PAIR), lambda g, h: (g, 0, h))
    shape = jax.ShapeDtypeStruct(arrays[0].shape, jnp.bfloat16)
    return pl.pallas_call(
        kernel,
        grid=(groups, width // PAIR),
        in_specs=[pl.BlockSpec((1, 1, seq_len), lambda g, h: (g, 0, 0))] + [block] * len(arrays),
        out_specs=[block] * outputs,
        out_shape=[shape] * outputs,
    )(key_keep[:, None, :], *arrays)


def fold_table(one_hot, per_image):
    return jnp.einsum("gi,gdr->idr", one_hot, per_image)


def gather_rows(rows):
    part = rows.shape[0] // lax.axis_size("seq")
    mine = lax.dynamic_slice_in_dim(rows, lax.axis_index("seq") * part, part, 0)
    return lax.all_gather(mine, ("dp", "seq"), axis=0, tiled=True)


def to_images(values):
    return lax.all_to_all(values, "seq", split_axis=0, concat_axis=1, tiled=True)


def to_tokens(values):
    return lax.all_to_all(values, "seq", split_axis=1, concat_axis=0, tiled=True)


def per_device(
    tokens,
    keep,
    adapter_id,
    w_qkv,
    w_o,
    w_up,
    w_down,
    ln1_gain,
    ln2_gain,
    qkv_in,
    qkv_out,
    o_in,
    o_out,
    up_in,
    up_out,
    down_in,
    down_out,
    cotangent,
):
    full_qkv = gather_rows(w_qkv)
    full_o = gather_rows(w_o)
    full_up = gather_rows(w_up)
    full_down = gather_rows(w_down)
    model_width = tokens.shape[2]
    tokens = to_images(tokens)
    cotangent = to_images(cotangent)
    groups = tokens.shape[0]
    first = lax.axis_index("seq") * groups
    keep_all = lax.dynamic_slice_in_dim(keep, first, groups, 0).astype(jnp.float32)
    adapter_id = lax.dynamic_slice_in_dim(adapter_id, first, groups, 0)
    keep_local = keep_all[:, :, None]
    sel_qkv_in = jnp.take(qkv_in, adapter_id, axis=1)
    sel_qkv_out = jnp.take(qkv_out, adapter_id, axis=1)
    sel_o_in = jnp.take(o_in, adapter_id, axis=0)
    sel_o_out = jnp.take(o_out, adapter_id, axis=0)
    sel_up_in = jnp.take(up_in, adapter_id, axis=0)
    sel_up_out = jnp.take(up_out, adapter_id, axis=0)
    sel_down_in = jnp.take(down_in, adapter_id, axis=0)
    sel_down_out = jnp.take(down_out, adapter_id, axis=0)
    tokens_f = tokens.astype(jnp.float32)
    normed = normalize(tokens_f, ln1_gain).astype(jnp.bfloat16)
    projected = []
    reduced_qkv = []
    for column in range(3):
        block_cols = full_qkv[:, column * model_width : (column + 1) * model_width]
        projection, reduced = adapted(normed, block_cols, sel_qkv_in[column], sel_qkv_out[column])
        projected.append(projection.astype(jnp.bfloat16))
        reduced_qkv.append(reduced)
    (mixed,) = attention_call(attend_kernel, keep_all, projected, 1)
    proj_o, reduced_o = adapted(mixed, full_o, sel_o_in, sel_o_out)
    after_attn = tokens_f + proj_o
    normed_two = normalize(after_attn, ln2_gain).astype(jnp.bfloat16)
    pre_act, reduced_up = adapted(normed_two, full_up, sel_up_in, sel_up_out)
    activated = jax.nn.gelu(pre_act, approximate=False).astype(jnp.bfloat16)
    proj_down, reduced_down = adapted(activated, full_down, sel_down_in, sel_down_out)
    layer_out = ((after_attn + proj_down) * keep_local).astype(jnp.bfloat16)
    one_hot = (adapter_id[:, None] == jnp.arange(qkv_in.shape[1], dtype=jnp.int32)[None, :]).astype(
        jnp.float32
    )
    grad_layer = cotangent.astype(jnp.float32) * keep_local
    grad_down = grad_layer.astype(jnp.bfloat16)
    grad_activated, down_first, down_second = adapted_back(
        activated, full_down, sel_down_in, sel_down_out, reduced_down, grad_down
    )
    gelu_value, gelu_pull = jax.vjp(partial(jax.nn.gelu, approximate=False), pre_act)
    grad_pre = gelu_pull(grad_activated)[0].astype(jnp.bfloat16)
    grad_normed_two, up_first, up_second = adapted_back(
        normed_two, full_up, sel_up_in, sel_up_out, reduced_up, grad_pre
    )
    mlp_tables = (
        fold_table(one_hot, up_first),
        fold_table(one_hot, up_second),
        fold_table(one_hot, down_first),
        fold_table(one_hot, down_second),
    )
    norm_value, norm_two_pull = jax.vjp(partial(normalize, gains=ln2_gain), after_attn)
    grad_attn = grad_layer + norm_two_pull(grad_normed_two)[0]
    grad_proj = grad_attn.astype(jnp.bfloat16)
    grad_mixed, o_first, o_second = adapted_back(
        mixed, full_o, sel_o_in, sel_o_out, reduced_o, grad_proj
    )
    out_tables = (fold_table(one_hot, o_first), fold_table(one_hot, o_second))
    early = lax.psum(mlp_tables + out_tables, ("dp", "seq"))
    grad_projected = attention_call(
        attend_back_kernel, keep_all, (*projected, grad_mixed.astype(jnp.bfloat16)), 3
    )
    grad_normed = jnp.zeros(tokens.shape, jnp.float32)
    qkv_first = []
    qkv_second = []
    for column in range(3):
        block_cols = full_qkv[:, column * model_width : (column + 1) * model_width]
        grad_part, first_part, second_part = adapted_back(
            normed,
            block_cols,
            sel_qkv_in[column],
            sel_qkv_out[column],
            reduced_qkv[column],
            grad_projected[column],
        )
        grad_normed = grad_normed + grad_part
        qkv_first.append(fold_table(one_hot, first_part))
        qkv_second.append(fold_table(one_hot, second_part))
    norm_one_value, norm_one_pull = jax.vjp(partial(normalize, gains=ln1_gain), tokens_f)
    grad_input = (grad_attn + norm_one_pull(grad_normed)[0]).astype(jnp.bfloat16)
    qkv_tables = (jnp.stack(qkv_first, 0), jnp.stack(qkv_second, 0))
    qkv_tables, early = lax.optimization_barrier((qkv_tables, early))
    late = lax.psum(qkv_tables, ("dp", "seq"))
    return (to_tokens(layer_out), to_tokens(grad_input), *late, *early[4:], *early[:4])


def solution(mesh):
    return jax.shard_map(
        per_device,
        mesh=mesh,
        in_specs=(
            P("dp", "seq", None),
            P("dp", None),
            P("dp"),
            P("dp", None),
            P("dp", None),
            P("dp", None),
            P("dp", None),
            P(),
            P(),
            P(),
            P(),
            P(),
            P(),
            P(),
            P(),
            P(),
            P(),
            P("dp", "seq", None),
        ),
        out_specs=(
            P("dp", "seq", None),
            P("dp", "seq", None),
            P(),
            P(),
            P(),
            P(),
            P(),
            P(),
            P(),
            P(),
        ),
        check_vma=False,
    )
```

time: 828 us -> 755 us (0.912)
  local copies, waits for them, and re-layouts: 129 us -> 59.8 us
  Pallas kernels: 0 us -> 46.4 us
  matrix products: 180 us -> 140 us
  starting transfers between devices: 45.4 us -> 20.8 us
  waiting for transfers between devices: 390 us -> 414 us
  other arithmetic: 56.4 us -> 44.5 us
    psum x1 -> x2, waiting for transfers between devices: 166 us -> 240 us  [the longest x1 141 us: per_device(): early = lax.psum(mlp_tables + out_tables, ('dp', 'seq'))]
    dot_general x6 -> x0, matrix products: 50.1 us -> none  [the longest x1 10.8 us: masked_scores(): jnp.einsum('gqhc,gkhc->ghqk', head_q, head_k, preferred_element_type=jnp....]
    pallas_call x0 -> x2, Pallas kernels: none -> 46.4 us  [attention_call(): pl.pallas_call(kernel, grid=(groups, width // PAIR), in_specs=[pl.BlockSp...]
    all_to_all x12 -> x2, local copies, waits for them, and re-layouts: 46.9 us -> 4.25 us  [to_tokens(): lax.all_to_all(values, 'seq', split_axis=1, concat_axis=0, tiled=True)]
    reshape x8 -> x0, local copies, waits for them, and re-layouts: 28.9 us -> none  [the longest x4 17.6 us: split_heads(): return values.reshape(groups, seq_len, local_width // HEAD_DIM, HEAD_DIM)]
    all_to_all x8 -> x4, waiting for transfers between devices: 54.4 us -> 30.1 us  [the longest x2 18.9 us: to_tokens(): lax.all_to_all(values, 'seq', split_axis=1, concat_axis=0, tiled=True)]
    all_to_all x8 -> x4, starting transfers between devices: 44.7 us -> 20.4 us  [the longest x2 10.3 us: to_images(): lax.all_to_all(values, 'seq', split_axis=0, concat_axis=1, tiled=True)]
    all_gather x4, waiting for transfers between devices: 167 us -> 143 us  [gather_rows(): return lax.all_gather(mine, ('dp', 'seq'), axis=0, tiled=True)]
  transfers between devices with their start and end apart: 13 -> 10, of which waited for: 9 -> 8; matrix products, arithmetic and copies ran while one was open for 28% -> 22% of each run, Pallas kernels for 0% -> 3%
where the time goes in v1:
time: 755 us; the launch traced here: 741 us
  waiting for transfers between devices  414 us (55%)
  matrix products  140 us (19%)
  local copies, waits for them, and re-layouts  59.8 us (8%)
  Pallas kernels  46.4 us (6%)
  other arithmetic  44.5 us (6%)
  starting transfers between devices  20.8 us (3%)
  between operations  15.6 us (2%)
    all_gather x4, waiting for transfers between devices, gather_rows(): return lax.all_gather(mine, ('dp', 'seq'), axis=0, tiled=True)  143 us
    psum x1, waiting for transfers between devices, per_device(): early = lax.psum(mlp_tables + out_tables, ('dp', 'seq'))  141 us
    psum x1, waiting for transfers between devices, per_device(): late = lax.psum(qkv_tables, ('dp', 'seq'))  99.5 us
    pallas_call x2, Pallas kernels, attention_call(): pl.pallas_call(kernel, grid=(groups, width // PAIR), in_specs=[pl.BlockSp...  46.4 us
    dot_general x6, matrix products, adapted(): jnp.einsum('gld,de->gle', inputs, weight, preferred_element_type=jnp.floa...  33.5 us
    dot_general x6, matrix products, adapted_back(): jnp.einsum('gle,de->gld', upstream, weight, preferred_element_type=jnp.fl...  32.4 us
    convert_element_type x1, other arithmetic, per_device(): activated = jax.nn.gelu(pre_act, approximate=False).astype(jnp.bfloat16)  26.1 us
    unnamed x186, local copies, waits for them, and re-layouts  25 us
  transfers between devices with their start and end apart: 10, of which 8 were waited for; matrix products, arithmetic and copies ran while one was open for 22% of the time, Pallas kernels for 3%

profile of v1, /device:TPU:31, one launch (start us, length us, event | category | flops | bytes accessed | tf_op | source)
XLA Modules:
  0.0 741.2 jit_solution(4502145975928001278)
XLA Ops:
  11.4 4.3 all-to-all-start
  19.4 2.4 gather_fusion.1
  26.3 1.8 gather_fusion.2
  28.7 2.1 gather_fusion.7
  32.6 6.0 all-to-all-start.2
  39.0 2.6 copy.54
  43.2 2.2 fusion.18
  48.6 11.2 %all-to-all-done.2 = bf16[8,80,1024]{2,1,0:T(8,128)(2,1)} async-done(((bf16[8,80,1024]{2,1,0:T(8,128)(2,1)}), bf16[8,80,1024]{2,1,0:T(8,128)(2,1)}, u32[]{:S(2)}, u32[]{:S(2)}) %all-to-all-start.2) | async-done | bytes 1310752 | tf_op jit(solution)/shard_map/all_to_all | solution.py:117
  68.2 16.7 %all-gather.5.cloned.1.call-done = bf16[1024,3072]{1,0:T(8,128)(2,1)} async-done(((bf16[32,3072]{1,0:T(8,128)(2,1)}), bf16[1024,3072]{1,0:T(8,128)(2,1)}) %all-gather.5.cloned.1.call-update) | async-done | bytes 6291472 | tf_op jit(solution)/shard_map/all_gather | solution.py:113
  85.0 3.7 fusion.31
  96.6 18.7 %shard_map.249 = bf16[2,320,1024]{2,1,0:T(8,128)(2,1)} custom-call(f32[2,1,320]{2,1,0:T(1,128)} %broadcast_in_dim.91.keep_ref, bf16[2,320,1024]{2,1,0:T(8,128)(2,1)} %add_convert_fusion.5.q_ref, bf16[2,320,1024]{2,1,0:T(8,128)(2,1)} %add_convert_fusion.4.k_ref, bf16[2,320,1024]{2,1,0:T(8,128)(2,1)} %add_convert_fusion.3.v_ref), custom_call_target="tpu_custom_call" | custom-call | tf_op jit(solution)/shard_map/pallas_call | solution.py:97
  115.3 2.4 convolution_convert_fusion.8
  117.7 25.9 %all-gather.7.cloned.1.call-done = bf16[1024,1024]{1,0:T(8,128)(2,1)} async-done(((bf16[32,1024]{1,0:T(8,128)(2,1)}), bf16[1024,1024]{1,0:T(8,128)(2,1)}) %all-gather.7.cloned.1.call-update) | async-done | bytes 2097168 | tf_op jit(solution)/shard_map/all_gather | solution.py:113
  143.6 3.5 fusion.24
  151.8 5.5 fusion.58
  157.3 65.5 %all-gather.9.cloned.1.call-done = bf16[1024,4096]{1,0:T(8,128)(2,1)} async-done(((bf16[32,4096]{1,0:T(8,128)(2,1)}), bf16[1024,4096]{1,0:T(8,128)(2,1)}) %all-gather.9.cloned.1.call-update) | async-done | bytes 8388624 | tf_op jit(solution)/shard_map/all_gather | solution.py:113
  222.7 17.6 %fusion.20 = (u8[320,4096]{1,0:T(8,128)(4,1)S(1)}, u8[320,4096]{1,0:T(8,128)(4,1)S(1)}, f32[2,320,4096]{2,1,0:T(8,128)}) fusion(f32[2,320,4096]{2,1,0:T(8,128)} %fusion.58, bf16[2,320,1024]{2,1,0:T(8,128)(2,1)} %copy-done.15, bf16[1024,4096]{1,0:T(8,128)(2,1)} %all-gather.9.cloned.1.call-done), kind=kOutput, calls=%fused_computation.61 | convolution fusion | flops 5402787840 | bytes 33292288 | tf_op jit(solution)/shard_map/gld,de->gle/dot_general | solution.py:21
  240.3 26.1 %multiply_convert_fusion = (bf16[2,320,4096]{2,1,0:T(8,128)(2,1)}, f32[2,320,4096]{2,1,0:T(8,128)}) fusion(f32[2,320,4096]{2,1,0:T(8,128)} %get-tuple-element.82, u8[320,4096]{1,0:T(8,128)(4,1)S(1)} %get-tuple-element.65, u8[320,4096]{1,0:T(8,128)(4,1)S(1)} %get-tuple-element.64), kind=kLoop, calls=%fused_computation.16 | loop fusion | flops 183500800 | bytes 28835840 | tf_op jit(solution)/shard_map/convert_element_type | solution.py:178
  266.4 35.3 %all-gather.11.cloned.1.call-done = bf16[4096,1024]{1,0:T(8,128)(2,1)} async-done(((bf16[128,1024]{1,0:T(8,128)(2,1)}), bf16[4096,1024]{1,0:T(8,128)(2,1)}) %all-gather.11.cloned.1.call-update) | async-done | bytes 8388624 | tf_op jit(solution)/shard_map/all_gather | solution.py:113
  301.7 12.3 %fusion.6 = f32[2,320,4096]{2,1,0:T(8,128)} fusion(bf16[2,320,1024]{2,1,0:T(8,128)(2,1)} %copy-done.17, bf16[4096,1024]{1,0:T(8,128)(2,1)} %all-gather.11.cloned.1.call-done), kind=kOutput, calls=%fused_computation.29 | convolution fusion | flops 5368709120 | bytes 20185088 | tf_op jit(solution)/shard_map/gle,de->gld/dot_general | solution.py:39
  314.1 12.6 %add_convert_fusion = bf16[2,320,4096]{2,1,0:T(8,128)(2,1)S(1)} fusion(f32[2,320,4096]{2,1,0:T(8,128)} %get-tuple-element.77, f32[2,320,4096]{2,1,0:T(8,128)} %fusion.6, f32[2,320,4096]{2,1,0:T(8,128)} %get-tuple-element.82, bf16[2,320,16]{1,2,0:T(8,128)(2,1)S(1)} %copy-done.46, bf16[2,4096,16]{1,2,0:T(8,128)(2,1)S(1)} %gather_fusion.3, ...), kind=kOutput, calls=%fused_computation.15 | convolution fusion | flops 123338752 | bytes 36982784 | tf_op jit(solution)/shard_map/glr,gdr->gld/dot_general | solution.py:40
  330.2 8.4 %multiply_reduce_fusion.1 = (f32[2,320]{1,0:T(2,128)S(1)}, f32[2,320,1024]{2,1,0:T(8,128)S(1)}) fusion(f32[2,320,1024]{2,1,0:T(8,128)S(1)} %copy-done.7, f32[2,320]{1,0:T(2,128)S(1)} %copy-done.71, f32[1024]{0:T(1024)S(1)} %copy-done.81, f32[2,320,1024]{2,1,0:T(8,128)S(1)} %fusion.61, bf16[2,320,4096]{2,1,0:T(8,128)(2,1)S(1)} %add_convert_fusion, ...), kind=kOutput, calls=%fused_computation.50 | convolution fusion | flops 5371985408 | bytes 21505024 | tf_op jit(solution)/shard_map/gle,de->gld/dot_general | solution.py:39
  345.4 27.7 %shard_map.250 = (bf16[2,320,1024]{2,1,0:T(8,128)(2,1)}, bf16[2,320,1024]{2,1,0:T(8,128)(2,1)}, bf16[2,320,1024]{2,1,0:T(8,128)(2,1)}) custom-call(f32[2,1,320]{2,1,0:T(1,128)} %broadcast_in_dim.91.keep_ref, bf16[2,320,1024]{2,1,0:T(8,128)(2,1)} %add_convert_fusion.5.q_ref, bf16[2,320,1024]{2,1,0:T(8,128)(2,1)} %add_convert_fusion.4.k_ref, ...), custom_call_target="tpu_custom_call" | custom-call | tf_op jit(solution)/shard_map/pallas_call | solution.py:97
  373.1 1.9 convolution_convert_fusion.1
  375.0 2.9 fusion.60
  382.2 3.5 fusion.106
  392.7 5.7 multiply_convert_fusion.1
  398.4 2.4 copy.57
  400.8 5.6 all-to-all-start.1
  406.6 1.9 convolution_convert_fusion.2
  411.3 2.0 convolution_bitcast_fusion.4
  418.1 1.9 fusion.40
  420.0 1.9 fusion.38
  425.3 2.5 pad_maximum_fusion
  427.9 3.6 fusion.34
  432.8 3.2 fusion.32
  436.1 3.3 fusion.30
  444.5 140.7 %all-reduce.7.cloned.1.call-done = (f32[8,1024,16]{1,0,2:T(8,128)}, f32[8,16,4096]{2,0,1:T(8,128)}, f32[8,4096,16]{1,0,2:T(8,128)}, f32[8,16,1024]{2,0,1:T(8,128...) async-done(((f32[8,1024,16]{1,0,2:T(8,128)}, f32[8,16,4096]{2,0,1:T(8,128)}, f32[8,4096,16]{1,0,2:T(8,128)}, f32[8,16,1024]{2,0,1:T(8,128)}, f32[8,1024,16]{1,0,2:T(8,128)}, ...) | async-done | bytes 6291472 | tf_op jit(solution)/shard_map/psum | solution.py:207
  585.2 3.9 add_convert_fusion.1
  589.1 2.4 copy.60
  591.5 4.5 all-to-all-start.3
  596.0 2.8 copy.58
  598.9 18.9 %all-to-all-done.3 = bf16[2,320,1024]{2,0,1:T(2,128)(2,1)S(1)} async-done(((bf16[2,320,1024]{2,0,1:T(2,128)(2,1)}), bf16[2,320,1024]{2,0,1:T(2,128)(2,1)S(1)}, u32[]{:S(2)}, u32[]{:S(2)}) %all-to-all-start.3) | async-done | bytes 1310752 | tf_op jit(solution)/shard_map/all_to_all | solution.py:121
  622.5 2.5 copy.79
  625.1 2.5 copy.80
  628.7 99.5 %all-reduce.5.cloned.1.call-done = (f32[3,8,1024,16]{2,1,3,0:T(8,128)}, f32[3,8,16,1024]{3,1,2,0:T(8,128)}) async-done(((f32[3,8,1024,16]{2,1,3,0:T(8,128)}, f32[3,8,16,1024]{3,1,2,0:T(8,128)}), (f32[3,8,1024,16]{2,1,3,0:T(8,128)}, f32[3,8,16,1024]{3,1,2,0:T(8,128)})) %all-reduce.5.cloned.1.call-update) | async-done | bytes 3145744 | tf_op jit(solution)/shard_map/psum | solution.py:231
  728.3 3.6 copy.74
  731.9 2.1 copy.75
  (278 shorter events, 85.5 us)
Async XLA Ops:
  7.2 11.6 %copy-start.82 = (s32[8]{0:T(128)S(1)}, s32[8]{0:T(128)}, u32[]{:S(2)}) copy-start(s32[8]{0:T(128)} %param.24) | copy-start | bytes 100
  7.2 11.6 %copy-start.29 = (bf16[3,8,1024,16]{2,3,1,0:T(8,128)(2,1)S(1)}, bf16[3,8,1024,16]{2,3,1,0:T(8,128)(2,1)}, u32[]{:S(2)}) copy-start(bf16[3,8,1024,16]{2,3,1,0:T(8,128)(2,1)} %param.31) | copy-start | bytes 2359300
  7.2 77.8 %all-gather.5.cloned.1.call-start = ((), (), s32[]{:S(2)}) async-start(), calls=%async_computation.4 | async-start | bytes 6488064 | tf_op jit(solution)/shard_map/all_gather | solution.py:113
  9.0 134.5 %all-gather.7.cloned.1.call-start = ((), (), s32[]{:S(2)}) async-start(), calls=%async_computation.5 | async-start | bytes 2162688 | tf_op jit(solution)/shard_map/all_gather | solution.py:113
  10.6 212.2 %all-gather.9.cloned.1.call-start = ((), (), s32[]{:S(2)}) async-start(), calls=%async_computation.6 | async-start | bytes 8650752 | tf_op jit(solution)/shard_map/all_gather | solution.py:113
  11.4 21.2 %all-to-all-start = ((bf16[8,80,1024]{2,1,0:T(8,128)(2,1)}), bf16[8,80,1024]{2,1,0:T(8,128)(2,1)S(1)}, u32[]{:S(2)}, u32[]{:S(2)}) async-start(bf16[8,80,1024]{2,1,0:T(8,128)(2,1)} %param.22), calls=%async_computation | async-start | bytes 2621440 | tf_op jit(solution)/shard_map/all_to_all | solution.py:117
  15.7 286.0 %all-gather.11.cloned.1.call-start = ((), (), s32[]{:S(2)}) async-start(), calls=%async_computation.7 | async-start | bytes 8650752 | tf_op jit(solution)/shard_map/all_gather | solution.py:113
  18.9 9.3 %copy-start.28 = (bf16[8,4096,16]{1,2,0:T(8,128)(2,1)S(1)}, bf16[8,4096,16]{1,2,0:T(8,128)(2,1)}, u32[]{:S(2)}) copy-start(bf16[8,4096,16]{1,2,0:T(8,128)(2,1)} %param.37) | copy-start | bytes 3145732
  32.6 6.3 copy-start.22
  32.6 27.1 %all-to-all-start.2 = ((bf16[8,80,1024]{2,1,0:T(8,128)(2,1)}), bf16[8,80,1024]{2,1,0:T(8,128)(2,1)}, u32[]{:S(2)}, u32[]{:S(2)}) async-start(bf16[8,80,1024]{2,1,0:T(8,128)(2,1)} %param.39), calls=%async_computation.2 | async-start | bytes 2621440 | tf_op jit(solution)/shard_map/all_to_all | solution.py:117
  61.4 4.5 copy-start.9
  85.0 3.7 copy-start.55
  85.0 5.3 copy-start.83
  301.7 12.3 %copy-start.46 = (bf16[2,320,16]{1,2,0:T(8,128)(2,1)S(1)}, bf16[2,320,16]{1,2,0:T(8,128)(2,1)}, u32[]{:S(2)}) copy-start(bf16[2,320,16]{1,2,0:T(8,128)(2,1)} %convolution_convert_fusion.5) | copy-start | bytes 61444
  326.6 12.0 %copy-start.11 = (bf16[2,320,4096]{2,1,0:T(8,128)(2,1)}, bf16[2,320,4096]{2,1,0:T(8,128)(2,1)S(1)}, u32[]{:S(2)}) copy-start(bf16[2,320,4096]{2,1,0:T(8,128)(2,1)S(1)} %add_convert_fusion) | copy-start | bytes 15728644
  328.1 10.5 %copy-start.53 = (bf16[2,320,16]{1,2,0:T(8,128)(2,1)}, bf16[2,320,16]{1,2,0:T(8,128)(2,1)S(1)}, u32[]{:S(2)}) copy-start(bf16[2,320,16]{1,2,0:T(8,128)(2,1)S(1)} %convolution_convert_fusion.4) | copy-start | bytes 61444
  330.2 8.5 %copy-start.77 = (f32[2,320]{1,0:T(2,128)S(1)}, f32[2,320]{1,0:T(2,128)}, u32[]{:S(2)}) copy-start(f32[2,320]{1,0:T(2,128)} %copy-done.76) | copy-start | bytes 7684
  330.2 8.5 %copy-start.75 = (f32[2,320]{1,0:T(2,128)S(1)}, f32[2,320]{1,0:T(2,128)}, u32[]{:S(2)}) copy-start(f32[2,320]{1,0:T(2,128)} %copy-done.74) | copy-start | bytes 7684
  373.1 4.8 copy-start.4
  373.1 5.8 copy-start.27
  375.0 4.9 copy-start.60
  380.2 5.4 slice-start
  382.2 3.5 slice-start.1
  382.2 10.5 %slice-start.2 = ((s8[8388608]{0:T(1024)(128)(4,1)}), s8[4194304]{0:T(1024)(128)(4,1)S(1)}, s32[]{:S(2)}) async-start(s8[8388608]{0:T(1024)(128)(4,1)} %bitcast.209), calls=%async_computation.12 | async-start | bytes 8388608
  387.2 5.4 slice-start.3
  388.2 3.5 copy-start.21
  400.8 190.7 %all-to-all-start.1 = ((bf16[2,320,1024]{2,0,1:T(2,128)(2,1)}), bf16[2,320,1024]{2,0,1:T(2,128)(2,1)}, u32[]{:S(2)}, u32[]{:S(2)}) async-start(bf16[2,320,1024]{2,0,1:T(2,128)(2,1)} %copy.57), calls=%async_computation.1 | async-start | bytes 2621440 | tf_op jit(solution)/shard_map/all_to_all | solution.py:121
  406.4 178.8 %all-reduce.7.cloned.1.call-start = ((), (), s32[]{:S(2)}) async-start(), calls=%async_computation.9 | async-start | bytes 12582912 | tf_op jit(solution)/shard_map/psum | solution.py:207
  406.6 6.7 copy-start.5
  408.5 8.5 %copy-start.62 = (bf16[2,320,16]{1,2,0:T(8,128)(2,1)}, bf16[2,320,16]{1,2,0:T(8,128)(2,1)S(1)}, u32[]{:S(2)}) copy-start(bf16[2,320,16]{1,2,0:T(8,128)(2,1)S(1)} %convolution_convert_fusion.2) | copy-start | bytes 61444
  408.5 7.4 copy-start.48
  408.5 8.5 %copy-start.49 = (bf16[2,1024,16]{1,2,0:T(8,128)(2,1)S(1)}, bf16[2,1024,16]{1,2,0:T(8,128)(2,1)}, u32[]{:S(2)}) copy-start(bf16[2,1024,16]{1,2,0:T(8,128)(2,1)} %fusion.112) | copy-start | bytes 196612
  417.0 5.0 copy-start.50
  418.1 5.0 copy-start.51
  418.1 6.1 copy-start.52
  420.0 5.3 copy-start.34
  427.8 3.7 copy-start.36
  427.8 3.7 copy-start.63
  427.9 300.4 %all-reduce.5.cloned.1.call-start = ((), (), s32[]{:S(2)}) async-start(), calls=%async_computation.8 | async-start | bytes 6291456 | tf_op jit(solution)/shard_map/psum | solution.py:231
  443.1 142.1 %copy-start.73 = (f32[2,320]{1,0:T(2,128)S(1)}, f32[2,320]{1,0:T(2,128)}, u32[]{:S(2)}) copy-start(f32[2,320]{1,0:T(2,128)} %copy-done.72) | copy-start | bytes 7684
  591.5 26.3 %all-to-all-start.3 = ((bf16[2,320,1024]{2,0,1:T(2,128)(2,1)}), bf16[2,320,1024]{2,0,1:T(2,128)(2,1)S(1)}, u32[]{:S(2)}, u32[]{:S(2)}) async-start(bf16[2,320,1024]{2,0,1:T(2,128)(2,1)} %copy.60), calls=%async_computation.3 | async-start | bytes 2621440 | tf_op jit(solution)/shard_map/all_to_all | solution.py:121
  596.0 23.2 %copy-start.45 = (f32[8,1024,16]{1,0,2:T(8,128)S(1)}, f32[8,1024,16]{1,0,2:T(8,128)}, u32[]{:S(2)}) copy-start(f32[8,1024,16]{1,0,2:T(8,128)} %get-tuple-element.58) | copy-start | bytes 1572868
  596.0 24.3 %copy-start.44 = (f32[8,16,1024]{2,0,1:T(8,128)S(1)}, f32[8,16,1024]{2,0,1:T(8,128)}, u32[]{:S(2)}) copy-start(f32[8,16,1024]{2,0,1:T(8,128)} %get-tuple-element.59) | copy-start | bytes 1572868
  598.9 22.6 %copy-start.43 = (f32[8,1024,16]{1,0,2:T(8,128)S(1)}, f32[8,1024,16]{1,0,2:T(8,128)}, u32[]{:S(2)}) copy-start(f32[8,1024,16]{1,0,2:T(8,128)} %get-tuple-element.60) | copy-start | bytes 1572868
  617.8 4.7 copy-start.31
  621.4 3.6 copy-start.30
  728.3 3.6 copy-start.37
  728.3 5.7 copy-start.1
  (51 other events, 104.4 us)
Sparse Core Ops, SparseCore 0:
  11.5 73.4 all-gather.4
  88.4 55.1 all-gather.6
  147.0 75.6 all-gather.8
  226.0 75.6 all-gather.10
  428.0 157.1 all-reduce.6
  591.2 136.9 all-reduce.4

commit v2 on v1

--- a/solution.py
+++ b/solution.py
@@ -4,6 +4,7 @@
 import jax.numpy as jnp
 from jax import lax
 from jax.experimental import pallas as pl
+from jax.experimental.pallas import tpu as pltpu
 from jax.sharding import PartitionSpec as P
 
 HEAD_DIM = 64
@@ -34,7 +35,7 @@
     ).astype(jnp.bfloat16)
     grad_second = jnp.einsum("glr,gle->gre", reduced, upstream, preferred_element_type=jnp.float32)
     grad_first = jnp.einsum(
-        "gld,glr->gdr", inputs, grad_reduced, preferred_element_type=jnp.float32
+        "gld,glr->grd", inputs, grad_reduced, preferred_element_type=jnp.float32
     )
     grad_inputs = jnp.einsum("gle,de->gld", upstream, weight, preferred_element_type=jnp.float32)
     grad_inputs = grad_inputs + jnp.einsum(
@@ -103,8 +104,135 @@
     )(key_keep[:, None, :], *arrays)
 
 
-def fold_table(one_hot, per_image):
-    return jnp.einsum("gi,gdr->idr", one_hot, per_image)
+def exchange_kernel(send_ref, full_ref, received, total, send_one, recv_one, send_two, recv_two, pass_on):
+    count, groups, _, _ = send_ref.shape
+    adapters, rows = total.shape[:2]
+    dp, seq = lax.axis_index("dp"), lax.axis_index("seq")
+    width = lax.axis_size("seq")
+    me = dp * width + seq
+    core = seq % 2
+    sibling = me + 1 - 2 * core
+    chips = count // 2
+
+    def slice_to(target, source):
+        return pltpu.make_async_remote_copy(
+            send_ref.at[target],
+            received.at[source],
+            send_one.at[target],
+            recv_one.at[source],
+            device_id={"dp": target // width, "seq": target % width},
+            device_id_type=pl.DeviceIdType.MESH,
+        )
+
+    def start_slice(step, carry):
+        slice_to((me + step) % count, me).start()
+        return carry
+
+    lax.fori_loop(1, count, start_slice, 0)
+    received[me] = send_ref[me]
+    total[...] = jnp.zeros(total.shape, jnp.float32)
+
+    def add_slice(step, carry):
+        source = (me + count - step) % count
+
+        @pl.when(step > 0)
+        def _():
+            slice_to(me, source).wait_recv()
+
+        for group in range(groups):
+            hot = received[source, group, :16, :].astype(jnp.float32)
+            table = received[source, group, 16:, :].astype(jnp.float32)
+            for adapter in range(adapters):
+                total[adapter] = total[adapter] + hot[adapter : adapter + 1] * table
+        return carry
+
+    lax.fori_loop(0, count, add_slice, 0)
+    full_ref[me] = total[...].astype(jnp.bfloat16)
+
+    def block_to(target, block, sem):
+        return pltpu.make_async_remote_copy(
+            full_ref.at[block],
+            full_ref.at[block],
+            sem,
+            recv_two.at[block],
+            device_id={"dp": target // width, "seq": target % width},
+            device_id_type=pl.DeviceIdType.MESH,
+        )
+
+    def other_chip(step):
+        return ((me // 2 + step) % chips) * 2 + core
+
+    def start_block(step, carry):
+        target = other_chip(step)
+        block_to(target, me, send_two.at[target // 2]).start()
+        return carry
+
+    block_to(sibling, me, pass_on.at[me // 2]).start()
+    lax.fori_loop(1, chips, start_block, 0)
+
+    def relay(step, carry):
+        source = other_chip(chips - step)
+        block_to(sibling, source, send_two.at[source // 2]).wait_recv()
+        block_to(sibling, source, pass_on.at[source // 2]).start()
+        return carry
+
+    lax.fori_loop(1, chips, relay, 0)
+
+    def finish(step, carry):
+        source = other_chip(step)
+        theirs = source + 1 - 2 * core
+        block_to(sibling, theirs, pass_on.at[source // 2]).wait_recv()
+        block_to(sibling, source, pass_on.at[source // 2]).wait_send()
+        return carry
+
+    lax.fori_loop(0, chips, finish, 0)
+
+    def sent_block(step, carry):
+        target = other_chip(step)
+        block_to(target, me, send_two.at[target // 2]).wait_send()
+        return carry
+
+    lax.fori_loop(1, chips, sent_block, 0)
+
+    def sent_slice(step, carry):
+        slice_to((me + step) % count, me).wait_send()
+        return carry
+
+    lax.fori_loop(1, count, sent_slice, 0)
+
+
+def sum_tables(tables, one_hot):
+    groups, rows, columns = tables.shape
+    adapters = one_hot.shape[1]
+    count = lax.axis_size("dp") * lax.axis_size("seq")
+    across = columns // 128
+    down = count // across
+    part = rows // down
+    padded = -(-part // 16) * 16
+    blocks = tables.astype(jnp.bfloat16).reshape(groups, down, part, across, 128)
+    blocks = blocks.transpose(1, 3, 0, 2, 4).reshape(count, groups, part, 128)
+    hot = jnp.pad(one_hot, ((0, 0), (0, 16 - adapters))).astype(jnp.bfloat16)
+    hot = jnp.broadcast_to(hot[None, :, :, None], (count, groups, 16, 128))
+    blocks = jnp.pad(blocks, ((0, 0), (0, 0), (0, padded - part), (0, 0)))
+    vmem = pl.BlockSpec(memory_space=pltpu.VMEM)
+    full = pl.pallas_call(
+        exchange_kernel,
+        in_specs=[vmem],
+        out_specs=vmem,
+        out_shape=jax.ShapeDtypeStruct((count, adapters, padded, 128), jnp.bfloat16),
+        scratch_shapes=[
+            pltpu.VMEM((count, groups, 16 + padded, 128), jnp.bfloat16),
+            pltpu.VMEM((adapters, padded, 128), jnp.float32),
+            pltpu.SemaphoreType.DMA((count,)),
+            pltpu.SemaphoreType.DMA((count,)),
+            pltpu.SemaphoreType.DMA((count // 2,)),
+            pltpu.SemaphoreType.DMA((count,)),
+            pltpu.SemaphoreType.DMA((count // 2,)),
+        ],
+        compiler_params=pltpu.CompilerParams(has_side_effects=True),
+    )(jnp.concatenate([hot, blocks], 2))
+    full = full[:, :, :part].reshape(down, across, adapters, part, 128)
+    return full.transpose(2, 0, 3, 1, 4).reshape(adapters, rows, columns)
 
 
 def gather_rows(rows):
@@ -141,8 +269,9 @@
     down_out,
     cotangent,
 ):
-    full_qkv = gather_rows(w_qkv)
-    full_o = gather_rows(w_o)
+    qkv_width = w_qkv.shape[1]
+    full_qkv_o = gather_rows(jnp.concatenate([w_qkv, w_o], 1))
+    full_qkv, full_o = full_qkv_o[:, :qkv_width], full_qkv_o[:, qkv_width:]
     full_up = gather_rows(w_up)
     full_down = gather_rows(w_down)
     model_width = tokens.shape[2]
@@ -191,20 +320,12 @@
     grad_normed_two, up_first, up_second = adapted_back(
         normed_two, full_up, sel_up_in, sel_up_out, reduced_up, grad_pre
     )
-    mlp_tables = (
-        fold_table(one_hot, up_first),
-        fold_table(one_hot, up_second),
-        fold_table(one_hot, down_first),
-        fold_table(one_hot, down_second),
-    )
     norm_value, norm_two_pull = jax.vjp(partial(normalize, gains=ln2_gain), after_attn)
     grad_attn = grad_layer + norm_two_pull(grad_normed_two)[0]
     grad_proj = grad_attn.astype(jnp.bfloat16)
     grad_mixed, o_first, o_second = adapted_back(
         mixed, full_o, sel_o_in, sel_o_out, reduced_o, grad_proj
     )
-    out_tables = (fold_table(one_hot, o_first), fold_table(one_hot, o_second))
-    early = lax.psum(mlp_tables + out_tables, ("dp", "seq"))
     grad_projected = attention_call(
         attend_back_kernel, keep_all, (*projected, grad_mixed.astype(jnp.bfloat16)), 3
     )
@@ -222,14 +343,30 @@
             grad_projected[column],
         )
         grad_normed = grad_normed + grad_part
-        qkv_first.append(fold_table(one_hot, first_part))
-        qkv_second.append(fold_table(one_hot, second_part))
+        qkv_first.append(first_part)
+        qkv_second.append(second_part)
     norm_one_value, norm_one_pull = jax.vjp(partial(normalize, gains=ln1_gain), tokens_f)
     grad_input = (grad_attn + norm_one_pull(grad_normed)[0]).astype(jnp.bfloat16)
-    qkv_tables = (jnp.stack(qkv_first, 0), jnp.stack(qkv_second, 0))
-    qkv_tables, early = lax.optimization_barrier((qkv_tables, early))
-    late = lax.psum(qkv_tables, ("dp", "seq"))
-    return (to_tokens(layer_out), to_tokens(grad_input), *late, *early[4:], *early[:4])
+    pieces = (
+        *qkv_first, *qkv_second, o_first, o_second, up_first, up_second, down_first, down_second
+    )
+    flat = [piece.reshape(groups, -1, model_width).astype(jnp.bfloat16) for piece in pieces]
+    summed = sum_tables(jnp.concatenate(flat, 1), one_hot)
+    tables = []
+    start = 0
+    for index, (piece, rows) in enumerate(zip(pieces, flat)):
+        stop = start + rows.shape[1]
+        table = summed[:, start:stop].reshape(-1, *piece.shape[1:]).astype(jnp.float32)
+        is_first = index < 3 or (index > 5 and index % 2 == 0)
+        tables.append(table.swapaxes(1, 2) if is_first else table)
+        start = stop
+    return (
+        to_tokens(layer_out),
+        to_tokens(grad_input),
+        jnp.stack(tables[:3]),
+        jnp.stack(tables[3:6]),
+        *tables[6:],
+    )
 
 
 def solution(mesh):

time: 755 us -> 574 us (0.76)
  waiting for transfers between devices: 414 us -> 112 us
  Pallas kernels: 46.4 us -> 173 us
  matrix products: 140 us -> 130 us
    psum x2 -> x0, waiting for transfers between devices: 240 us -> none  [the longest x1 141 us: per_device(): early = lax.psum(mlp_tables + out_tables, ('dp', 'seq'))]
    pallas_call x0 -> x1, Pallas kernels: none -> 127 us  [sum_tables(): pl.pallas_call(exchange_kernel, in_specs=[vmem], out_specs=vmem, out_shap...]
    all_gather x4 -> x3, waiting for transfers between devices: 143 us -> 95.8 us  [gather_rows(): return lax.all_gather(mine, ('dp', 'seq'), axis=0, tiled=True)]
    all_to_all x2, waiting for transfers between devices: 18.9 us -> 0.01 us  [to_tokens(): lax.all_to_all(values, 'seq', split_axis=1, concat_axis=0, tiled=True)]
    dot_general x18 -> x6, matrix products: 20.8 us -> 5.64 us  [adapted_back(): jnp.einsum('gld,glr->grd', inputs, grad_reduced, preferred_element_type=j...]
    unnamed x186 -> x131, local copies, waits for them, and re-layouts: 25 us -> 12.4 us
    transpose x0 -> x3, local copies, waits for them, and re-layouts: none -> 9.72 us  [the longest x1 7.64 us: sum_tables(): return full.transpose(2, 0, 3, 1, 4).reshape(adapters, rows, columns)]
    reshape x0 -> x1, local copies, waits for them, and re-layouts: none -> 8.16 us  [sum_tables(): return full.transpose(2, 0, 3, 1, 4).reshape(adapters, rows, columns)]
  transfers between devices with their start and end apart: 10 -> 7, of which waited for: 8 -> 4; matrix products, arithmetic and copies ran while one was open for 22% -> 30% of each run, Pallas kernels for 3% -> 26%
where the time goes in v2:
time: 574 us; the launch traced here: 566 us
  Pallas kernels  173 us (30%)
  matrix products  130 us (23%)
  waiting for transfers between devices  112 us (20%)
  local copies, waits for them, and re-layouts  65.8 us (11%)
  other arithmetic  49.8 us (9%)
  starting transfers between devices  19.6 us (3%)
  between operations  15.1 us (3%)
    pallas_call x1, Pallas kernels, sum_tables(): pl.pallas_call(exchange_kernel, in_specs=[vmem], out_specs=vmem, out_shap...  127 us
    all_gather x3, waiting for transfers between devices, gather_rows(): return lax.all_gather(mine, ('dp', 'seq'), axis=0, tiled=True)  95.8 us
    pallas_call x2, Pallas kernels, attention_call(): pl.pallas_call(kernel, grid=(groups, width // PAIR), in_specs=[pl.BlockSp...  46.3 us
    dot_general x6, matrix products, adapted_back(): jnp.einsum('gle,de->gld', upstream, weight, preferred_element_type=jnp.fl...  33.9 us
    dot_general x6, matrix products, adapted(): jnp.einsum('gld,de->gle', inputs, weight, preferred_element_type=jnp.floa...  33.5 us
    convert_element_type x1, other arithmetic, per_device(): activated = jax.nn.gelu(pre_act, approximate=False).astype(jnp.bfloat16)  26.2 us
    dot_general x6, matrix products, adapted_back(): jnp.einsum('glr,gdr->gld', grad_reduced, first_rank, preferred_element_ty...  19.8 us
    all_to_all x2, waiting for transfers between devices, to_images(): lax.all_to_all(values, 'seq', split_axis=0, concat_axis=1, tiled=True)  16.2 us
  transfers between devices with their start and end apart: 7, of which 4 were waited for; matrix products, arithmetic and copies ran while one was open for 30% of the time, Pallas kernels for 26%

profile of v2, /device:TPU:31, one launch (start us, length us, event | category | flops | bytes accessed | tf_op | source)
XLA Modules:
  0.0 565.5 jit_solution(2954291776559201891)
XLA Ops:
  7.3 1.8 fusion.48
  9.9 4.3 all-to-all-start
  14.2 1.7 constant_dynamic-slice_fusion
  17.9 2.4 gather_fusion.1
  24.8 1.8 gather_fusion.2
  27.2 2.1 gather_fusion.7
  31.7 5.9 %all-to-all-start.2 = ((bf16[8,80,1024]{2,1,0:T(8,128)(2,1)}), bf16[8,80,1024]{2,1,0:T(8,128)(2,1)}, u32[]{:S(2)}, u32[]{:S(2)}) async-start(bf16[8,80,1024]{2,1,0:T(8,128)(2,1)} %param.39), calls=%async_computation.2 | async-start | bytes 2621440 | tf_op jit(solution)/shard_map/all_to_all | solution.py:245
  37.9 2.6 copy.41
  40.9 2.2 fusion.19
  44.4 16.2 %all-to-all-done.2 = bf16[8,80,1024]{2,1,0:T(8,128)(2,1)} async-done(((bf16[8,80,1024]{2,1,0:T(8,128)(2,1)}), bf16[8,80,1024]{2,1,0:T(8,128)(2,1)}, u32[]{:S(2)}, u32[]{:S(2)}) %all-to-all-start.2) | async-done | bytes 1310752 | tf_op jit(solution)/shard_map/all_to_all | solution.py:245
  69.0 27.3 %all-gather.4.cloned.1.call-done = bf16[1024,4096]{1,0:T(8,128)(2,1)} async-done(((bf16[32,4096]{1,0:T(8,128)(2,1)}), bf16[1024,4096]{1,0:T(8,128)(2,1)}) %all-gather.4.cloned.1.call-update) | async-done | bytes 8388624 | tf_op jit(solution)/shard_map/all_gather | solution.py:241
  96.4 3.7 fusion.28
  108.0 18.7 %shard_map.249 = bf16[2,320,1024]{2,1,0:T(8,128)(2,1)} custom-call(f32[2,1,320]{2,1,0:T(1,128)} %broadcast_in_dim.97.keep_ref, bf16[2,320,1024]{2,1,0:T(8,128)(2,1)} %add_convert_fusion.5.q_ref, bf16[2,320,1024]{2,1,0:T(8,128)(2,1)} %add_convert_fusion.4.k_ref, bf16[2,320,1024]{2,1,0:T(8,128)(2,1)} %add_convert_fusion.3.v_ref), custom_call_target="tpu_custom_call" | custom-call | tf_op jit(solution)/shard_map/pallas_call | solution.py:98
  126.7 2.0 convolution_convert_fusion.20
  128.7 3.6 fusion.34
  137.0 5.5 fusion.51
  142.5 33.0 %all-gather.6.cloned.1.call-done = bf16[1024,4096]{1,0:T(8,128)(2,1)} async-done(((bf16[32,4096]{1,0:T(8,128)(2,1)}), bf16[1024,4096]{1,0:T(8,128)(2,1)}) %all-gather.6.cloned.1.call-update) | async-done | bytes 8388624 | tf_op jit(solution)/shard_map/all_gather | solution.py:241
  175.5 17.6 %fusion.21 = (u8[320,4096]{1,0:T(8,128)(4,1)S(1)}, u8[320,4096]{1,0:T(8,128)(4,1)S(1)}, f32[2,320,4096]{2,1,0:T(8,128)}) fusion(f32[2,320,4096]{2,1,0:T(8,128)} %fusion.51, bf16[2,320,1024]{2,1,0:T(8,128)(2,1)} %copy-done.16, bf16[1024,4096]{1,0:T(8,128)(2,1)} %all-gather.6.cloned.1.call-done), kind=kOutput, calls=%fused_computation.65 | convolution fusion | flops 5402787840 | bytes 33292288 | tf_op jit(solution)/shard_map/gld,de->gle/dot_general | solution.py:22
  193.1 26.2 %multiply_convert_fusion = (bf16[2,320,4096]{2,1,0:T(8,128)(2,1)}, f32[2,320,4096]{2,1,0:T(8,128)}) fusion(f32[2,320,4096]{2,1,0:T(8,128)} %get-tuple-element.40, u8[320,4096]{1,0:T(8,128)(4,1)S(1)} %get-tuple-element.19, u8[320,4096]{1,0:T(8,128)(4,1)S(1)} %get-tuple-element.18), kind=kLoop, calls=%fused_computation.16 | loop fusion | flops 183500800 | bytes 28835840 | tf_op jit(solution)/shard_map/convert_element_type | solution.py:307
  219.2 35.4 %all-gather.8.cloned.1.call-done = bf16[4096,1024]{1,0:T(8,128)(2,1)} async-done(((bf16[128,1024]{1,0:T(8,128)(2,1)}), bf16[4096,1024]{1,0:T(8,128)(2,1)}) %all-gather.8.cloned.1.call-update) | async-done | bytes 8388624 | tf_op jit(solution)/shard_map/all_gather | solution.py:241
  254.7 12.2 %fusion.6 = f32[2,320,4096]{2,1,0:T(8,128)} fusion(bf16[2,320,1024]{2,1,0:T(8,128)(2,1)} %copy-done.18, bf16[4096,1024]{1,0:T(8,128)(2,1)} %all-gather.8.cloned.1.call-done), kind=kOutput, calls=%fused_computation.29 | convolution fusion | flops 5368709120 | bytes 20185088 | tf_op jit(solution)/shard_map/gle,de->gld/dot_general | solution.py:40
  266.9 12.6 %add_convert_fusion = bf16[2,320,4096]{2,1,0:T(8,128)(2,1)S(1)} fusion(f32[2,320,4096]{2,1,0:T(8,128)} %get-tuple-element.23, f32[2,320,4096]{2,1,0:T(8,128)} %fusion.6, f32[2,320,4096]{2,1,0:T(8,128)} %get-tuple-element.40, bf16[2,320,16]{1,2,0:T(8,128)(2,1)S(1)} %copy-done.35, bf16[2,4096,16]{1,2,0:T(8,128)(2,1)S(1)} %gather_fusion.3, ...), kind=kOutput, calls=%fused_computation.15 | convolution fusion | flops 123338752 | bytes 36982784 | tf_op jit(solution)/shard_map/glr,gdr->gld/dot_general | solution.py:41
  283.0 8.6 %multiply_reduce_fusion.1 = (f32[2,320]{1,0:T(2,128)S(1)}, f32[2,320,1024]{2,1,0:T(8,128)S(1)}) fusion(f32[2,320,1024]{2,1,0:T(8,128)S(1)} %copy-done.7, f32[2,320]{1,0:T(2,128)S(1)} %copy-done.48, f32[1024]{0:T(1024)S(1)} %copy-done.56, f32[2,320,1024]{2,1,0:T(8,128)S(1)} %fusion.54, bf16[2,320,4096]{2,1,0:T(8,128)(2,1)S(1)} %add_convert_fusion, ...), kind=kOutput, calls=%fused_computation.54 | convolution fusion | flops 5371985408 | bytes 21505024 | tf_op jit(solution)/shard_map/gle,de->gld/dot_general | solution.py:40
  294.3 3.2 fusion.33
  299.1 27.6 %shard_map.250 = (bf16[2,320,1024]{2,1,0:T(8,128)(2,1)}, bf16[2,320,1024]{2,1,0:T(8,128)(2,1)}, bf16[2,320,1024]{2,1,0:T(8,128)(2,1)}) custom-call(f32[2,1,320]{2,1,0:T(1,128)} %broadcast_in_dim.97.keep_ref, bf16[2,320,1024]{2,1,0:T(8,128)(2,1)} %add_convert_fusion.5.q_ref, bf16[2,320,1024]{2,1,0:T(8,128)(2,1)} %add_convert_fusion.4.k_ref, ...), custom_call_target="tpu_custom_call" | custom-call | tf_op jit(solution)/shard_map/pallas_call | solution.py:98
  326.7 1.9 convolution_convert_fusion.14
  328.6 3.1 fusion.52
  332.6 3.5 convolution_convert_fusion.1
  340.3 5.6 multiply_convert_fusion.1
  346.0 2.4 copy.44
  348.4 5.8 %all-to-all-start.1 = ((bf16[2,320,1024]{2,0,1:T(2,128)(2,1)}), bf16[2,320,1024]{2,0,1:T(2,128)(2,1)}, u32[]{:S(2)}, u32[]{:S(2)}) async-start(bf16[2,320,1024]{2,0,1:T(2,128)(2,1)} %copy.44), calls=%async_computation.1 | async-start | bytes 2621440 | tf_op jit(solution)/shard_map/all_to_all | solution.py:249
  354.2 1.9 convolution_convert_fusion.12
  356.1 1.8 convolution_convert_fusion.13
  358.4 3.3 fusion.31
  361.8 3.3 fusion.29
  365.1 3.3 fusion.27
  374.1 2.4 copy.47
  382.5 2.3 fusion.43
  389.9 3.6 all-to-all-start.3
  394.9 127.1 %shard_map.251 = bf16[32,8,80,128]{3,2,1,0:T(8,128)(2,1)} custom-call(bf16[32,2,96,128]{3,2,1,0:T(8,128)(2,1)} %fusion.35.send_ref), custom_call_target="tpu_custom_call" | custom-call | tf_op jit(solution)/shard_map/pallas_call | solution.py:218
  522.0 2.3 slice-done.2
  524.4 7.6 %copy.50 = bf16[8,4,72,8,128]{4,3,2,1,0:T(8,128)(2,1)} copy(bf16[8,4,72,8,128]{4,2,0,3,1:T(8,128)(2,1)S(1)} %bitcast.202) | data formatting | bytes 9437184 | tf_op jit(solution)/shard_map/transpose | solution.py:235
  532.0 8.2 %reshape.139 = bf16[8,288,1024]{2,1,0:T(8,128)(2,1)} reshape(bf16[8,4,72,8,128]{4,3,2,1,0:T(8,128)(2,1)} %copy.50) | data formatting | bytes 9437184 | tf_op jit(solution)/shard_map/reshape | solution.py:235
  540.2 3.3 slice_convert_fusion
  543.5 3.2 reshape.142
  546.6 1.9 reshape.143
  548.6 3.2 slice_convert_fusion.2
  554.3 2.8 copy.45
  (217 shorter events, 68.8 us)
Async XLA Ops:
  7.2 89.2 %all-gather.4.cloned.1.call-start = ((), (), s32[]{:S(2)}) async-start(), calls=%async_computation.4 | async-start | bytes 8650752 | tf_op jit(solution)/shard_map/all_gather | solution.py:241
  7.2 8.7 %copy-start.58 = (s32[8]{0:T(128)S(1)}, s32[8]{0:T(128)}, u32[]{:S(2)}) copy-start(s32[8]{0:T(128)} %param.24) | copy-start | bytes 100
  7.3 10.1 %copy-start.28 = (bf16[3,8,1024,16]{2,3,1,0:T(8,128)(2,1)S(1)}, bf16[3,8,1024,16]{2,3,1,0:T(8,128)(2,1)}, u32[]{:S(2)}) copy-start(bf16[3,8,1024,16]{2,3,1,0:T(8,128)(2,1)} %param.31) | copy-start | bytes 2359300
  9.1 166.4 %all-gather.6.cloned.1.call-start = ((), (), s32[]{:S(2)}) async-start(), calls=%async_computation.5 | async-start | bytes 8650752 | tf_op jit(solution)/shard_map/all_gather | solution.py:241
  9.9 21.8 %all-to-all-start = ((bf16[8,80,1024]{2,1,0:T(8,128)(2,1)}), bf16[8,80,1024]{2,1,0:T(8,128)(2,1)S(1)}, u32[]{:S(2)}, u32[]{:S(2)}) async-start(bf16[8,80,1024]{2,1,0:T(8,128)(2,1)} %param.22), calls=%async_computation | async-start | bytes 2621440 | tf_op jit(solution)/shard_map/all_to_all | solution.py:245
  14.2 240.4 %all-gather.8.cloned.1.call-start = ((), (), s32[]{:S(2)}) async-start(), calls=%async_computation.6 | async-start | bytes 8650752 | tf_op jit(solution)/shard_map/all_gather | solution.py:241
  17.3 9.3 %copy-start.27 = (bf16[8,4096,16]{1,2,0:T(8,128)(2,1)S(1)}, bf16[8,4096,16]{1,2,0:T(8,128)(2,1)}, u32[]{:S(2)}) copy-start(bf16[8,4096,16]{1,2,0:T(8,128)(2,1)} %param.37) | copy-start | bytes 3145732
  31.7 6.2 %copy-start.22 = (bf16[8,80,1024]{2,1,0:T(8,128)(2,1)}, bf16[8,80,1024]{2,1,0:T(8,128)(2,1)S(1)}, u32[]{:S(2)}) copy-start(bf16[8,80,1024]{2,1,0:T(8,128)(2,1)S(1)} %all-to-all-done) | copy-start | bytes 3932164
  31.7 28.8 %all-to-all-start.2 = ((bf16[8,80,1024]{2,1,0:T(8,128)(2,1)}), bf16[8,80,1024]{2,1,0:T(8,128)(2,1)}, u32[]{:S(2)}, u32[]{:S(2)}) async-start(bf16[8,80,1024]{2,1,0:T(8,128)(2,1)} %param.39), calls=%async_computation.2 | async-start | bytes 2621440 | tf_op jit(solution)/shard_map/all_to_all | solution.py:245
  37.9 2.6 copy-start.13
  62.2 4.4 copy-start.9
  65.5 2.4 copy-start.31
  96.4 3.7 copy-start.43
  96.4 5.3 copy-start.59
  128.7 3.6 copy-start.45
  254.7 12.2 %copy-start.35 = (bf16[2,320,16]{1,2,0:T(8,128)(2,1)S(1)}, bf16[2,320,16]{1,2,0:T(8,128)(2,1)}, u32[]{:S(2)}) copy-start(bf16[2,320,16]{1,2,0:T(8,128)(2,1)} %convolution_convert_fusion.17) | copy-start | bytes 61444
  279.4 12.1 %copy-start.12 = (bf16[2,320,4096]{2,1,0:T(8,128)(2,1)}, bf16[2,320,4096]{2,1,0:T(8,128)(2,1)S(1)}, u32[]{:S(2)}) copy-start(bf16[2,320,4096]{2,1,0:T(8,128)(2,1)S(1)} %add_convert_fusion) | copy-start | bytes 15728644
  280.9 10.6 %copy-start.37 = (bf16[2,320,16]{1,2,0:T(8,128)(2,1)}, bf16[2,320,16]{1,2,0:T(8,128)(2,1)S(1)}, u32[]{:S(2)}) copy-start(bf16[2,320,16]{1,2,0:T(8,128)(2,1)S(1)} %convolution_convert_fusion.16) | copy-start | bytes 61444
  282.9 8.6 %copy-start.52 = (f32[2,320]{1,0:T(2,128)S(1)}, f32[2,320]{1,0:T(2,128)}, u32[]{:S(2)}) copy-start(f32[2,320]{1,0:T(2,128)} %copy-done.51) | copy-start | bytes 7684
  283.0 8.7 %copy-start.50 = (f32[2,320]{1,0:T(2,128)S(1)}, f32[2,320]{1,0:T(2,128)}, u32[]{:S(2)}) copy-start(f32[2,320]{1,0:T(2,128)} %copy-done.49) | copy-start | bytes 7684
  293.8 3.7 copy-start.21
  326.7 4.9 copy-start.4
  326.7 5.9 %copy-start.34 = (bf16[2,320,16]{1,2,0:T(8,128)(2,1)S(1)}, bf16[2,320,16]{1,2,0:T(8,128)(2,1)}, u32[]{:S(2)}) copy-start(bf16[2,320,16]{1,2,0:T(8,128)(2,1)} %copy-done.33) | copy-start | bytes 61444
  328.6 7.6 %slice-start = ((s8[5242880]{0:T(1024)(128)(4,1)}), s8[4194304]{0:T(1024)(128)(4,1)S(1)}, s32[]{:S(2)}) async-start(s8[5242880]{0:T(1024)(128)(4,1)} %bitcast.200), calls=%async_computation.7 | async-start | bytes 8388608
  332.6 3.5 slice-start.1
  332.6 6.6 %slice-start.3 = ((s8[8388608]{0:T(1024)(128)(4,1)}), s8[4194304]{0:T(1024)(128)(4,1)S(1)}, s32[]{:S(2)}) async-start(s8[8388608]{0:T(1024)(128)(4,1)} %bitcast.210), calls=%async_computation.10 | async-start | bytes 8388608
  336.1 3.0 slice-start.4
  348.4 41.5 %all-to-all-start.1 = ((bf16[2,320,1024]{2,0,1:T(2,128)(2,1)}), bf16[2,320,1024]{2,0,1:T(2,128)(2,1)}, u32[]{:S(2)}, u32[]{:S(2)}) async-start(bf16[2,320,1024]{2,0,1:T(2,128)(2,1)} %copy.44), calls=%async_computation.1 | async-start | bytes 2621440 | tf_op jit(solution)/shard_map/all_to_all | solution.py:249
  354.2 3.7 copy-start.30
  354.2 4.2 copy-start.24
  358.4 3.3 copy-start.25
  361.7 3.3 copy-start.26
  365.1 3.4 copy-start.23
  365.1 3.4 copy-start.54
  370.0 2.5 copy-start.15
  374.0 2.4 copy-start.5
  374.0 4.3 copy-start.44
  376.5 2.8 copy-start.42
  376.5 3.8 copy-start.40
  377.4 3.8 copy-start.20
  379.3 3.2 copy-start.46
  380.3 4.5 copy-start.17
  380.3 4.5 copy-start.38
  382.1 5.0 copy-start.19
  389.7 3.7 copy-start.57
  389.9 167.2 %all-to-all-start.3 = ((bf16[2,320,1024]{2,0,1:T(2,128)(2,1)}), bf16[2,320,1024]{2,0,1:T(2,128)(2,1)S(1)}, u32[]{:S(2)}, u32[]{:S(2)}) async-start(bf16[2,320,1024]{2,0,1:T(2,128)(2,1)} %copy.47), calls=%async_computation.3 | async-start | bytes 2621440 | tf_op jit(solution)/shard_map/all_to_all | solution.py:249
  522.0 2.3 slice-start.2
  554.3 4.3 copy-start.1
  (24 other events, 36.4 us)
Sparse Core Ops, SparseCore 0:
  11.4 84.8 all-gather.3
  99.8 75.6 all-gather.5
  178.9 75.6 all-gather.7

commit v3 on v1

--- a/solution.py
+++ b/solution.py
@@ -4,6 +4,7 @@
 import jax.numpy as jnp
 from jax import lax
 from jax.experimental import pallas as pl
+from jax.experimental.pallas import tpu as pltpu
 from jax.sharding import PartitionSpec as P
 
 HEAD_DIM = 64
@@ -34,7 +35,7 @@
     ).astype(jnp.bfloat16)
     grad_second = jnp.einsum("glr,gle->gre", reduced, upstream, preferred_element_type=jnp.float32)
     grad_first = jnp.einsum(
-        "gld,glr->gdr", inputs, grad_reduced, preferred_element_type=jnp.float32
+        "gld,glr->grd", inputs, grad_reduced, preferred_element_type=jnp.float32
     )
     grad_inputs = jnp.einsum("gle,de->gld", upstream, weight, preferred_element_type=jnp.float32)
     grad_inputs = grad_inputs + jnp.einsum(
@@ -103,8 +104,200 @@
     )(key_keep[:, None, :], *arrays)
 
 
-def fold_table(one_hot, per_image):
-    return jnp.einsum("gi,gdr->idr", one_hot, per_image)
+def tile_places(shapes):
+    return [
+        (table, row, column)
+        for table, (_, rows, columns) in enumerate(shapes)
+        for row in range(0, rows, 8)
+        for column in range(0, columns, 128)
+    ]
+
+
+def exchange_kernel(stacks, shapes, hot_ref, *refs):
+    tables, refs = refs[: len(shapes)], refs[len(shapes) :]
+    outputs, refs = refs[: len(stacks)], refs[len(stacks) :]
+    send_ref, received, total, full_ref = refs[:4]
+    send_one, recv_one, recv_two, send_z, send_y, send_x, send_c = refs[4:]
+    count, groups, chunk, _ = send_ref.shape
+    adapters = hot_ref.shape[1]
+    tiles = (chunk - adapters) // 8
+    dp, seq = lax.axis_index("dp"), lax.axis_index("seq")
+    width = lax.axis_size("seq")
+    columns = lax.axis_size("dp") // 2
+    me = dp * width + seq
+    high, low = dp // 2, dp % 2
+    seq_x = (seq + width // 2) % width
+    seq_c = seq + 1 - 2 * (seq % 2)
+    places = tile_places(shapes)
+
+    for target in range(count):
+        for group in range(groups):
+            mine = places[target * tiles : (target + 1) * tiles]
+            parts = [tables[t][group, r : r + 8, c : c + 128] for t, r, c in mine]
+            parts += [jnp.zeros((8, 128), jnp.float32)] * (tiles - len(mine))
+            parts.append(hot_ref[group])
+            send_ref[target, group] = jnp.concatenate(parts, 0).astype(jnp.bfloat16)
+
+    def remote(source_ref, target_ref, send_sem, recv_sem, target):
+        return pltpu.make_async_remote_copy(
+            source_ref,
+            target_ref,
+            send_sem,
+            recv_sem,
+            device_id={"dp": target // width, "seq": target % width},
+            device_id_type=pl.DeviceIdType.MESH,
+        )
+
+    def slice_to(target, source):
+        return remote(
+            send_ref.at[target],
+            received.at[source],
+            send_one.at[target],
+            recv_one.at[source],
+            target,
+        )
+
+    def loop(start, stop, body):
+        def step_body(step, carry):
+            body(step)
+            return carry
+
+        lax.fori_loop(start, stop, step_body, 0)
+
+    loop(1, count, lambda step: slice_to((me + step) % count, me).start())
+    received[me] = send_ref[me]
+    total[...] = jnp.zeros(total.shape, jnp.float32)
+
+    def add_slice(step):
+        source = (me + count - step) % count
+
+        @pl.when(step > 0)
+        def _():
+            slice_to(me, source).wait_recv()
+
+        for group in range(groups):
+            values = received[source, group].astype(jnp.float32)
+            hot = values[tiles * 8 :]
+            for tile in range(tiles):
+                table = values[tile * 8 : tile * 8 + 8]
+                for adapter in range(adapters):
+                    row = (tile * adapters + adapter) * 8
+                    total[row : row + 8] = total[row : row + 8] + hot[adapter : adapter + 1] * table
+
+    loop(0, count, add_slice)
+    full_ref[me] = total[...].astype(jnp.bfloat16)
+
+    def device(at_high, at_low, at_seq):
+        return (at_high * 2 + at_low) * width + at_seq
+
+    def block_to(target, block, sem):
+        return remote(full_ref.at[block], full_ref.at[block], sem, recv_two.at[block], target)
+
+    def along_z(step):
+        return block_to(device((high + step) % columns, low, seq), me, send_z.at[step])
+
+    def along_y(block):
+        return block_to(device(high, 1 - low, seq), block, send_y.at[block])
+
+    def along_x(block):
+        return block_to(device(high, low, seq_x), block, send_x.at[block])
+
+    def along_c(block):
+        return block_to(device(high, low, seq_c), block, send_c.at[block])
+
+    def in_column(step, at_low, at_seq):
+        return device((high + columns - step) % columns, at_low, at_seq)
+
+    loop(1, columns, lambda step: along_z(step).start())
+
+    def from_z(step):
+        block = in_column(step, low, seq)
+
+        @pl.when(step > 0)
+        def _():
+            along_y(block).wait_recv()
+
+        along_y(block).start()
+        along_x(block).start()
+        along_c(block).start()
+
+    def from_y(step):
+        block = in_column(step, 1 - low, seq)
+        along_x(block).wait_recv()
+        along_x(block).start()
+        along_c(block).start()
+
+    def from_x(at_low):
+        def body(step):
+            block = in_column(step, at_low, seq_x)
+            along_c(block).wait_recv()
+            along_c(block).start()
+
+        return body
+
+    def from_c(at_low, at_seq):
+        return lambda step: along_c(in_column(step, at_low, at_seq)).wait_recv()
+
+    loop(0, columns, from_z)
+    loop(0, columns, from_y)
+    loop(0, columns, from_x(low))
+    loop(0, columns, from_x(1 - low))
+    seq_xc = seq_x + 1 - 2 * (seq_x % 2)
+    for at_seq in (seq_c, seq_xc):
+        loop(0, columns, from_c(low, at_seq))
+        loop(0, columns, from_c(1 - low, at_seq))
+
+    for index, (table, row, column) in enumerate(places):
+        block, tile = index // tiles, index % tiles
+        start = tile * adapters * 8
+        values = full_ref[block, start : start + adapters * 8, :].astype(jnp.float32)
+        values = values.reshape(adapters, 8, 128)
+        output, place = next(
+            (n, table - first) for n, (first, size) in enumerate(stacks) if first <= table < first + size
+        )
+        outputs[output][place, :, row : row + 8, column : column + 128] = values
+
+    loop(1, columns, lambda step: along_z(step).wait_send())
+    loop(0, columns, lambda step: along_y(in_column(step, low, seq)).wait_send())
+    for at_low in (low, 1 - low):
+        loop(0, columns, lambda step: along_x(in_column(step, at_low, seq)).wait_send())
+        for at_seq in (seq, seq_x):
+            loop(0, columns, lambda step: along_c(in_column(step, at_low, at_seq)).wait_send())
+    loop(1, count, lambda step: slice_to((me + step) % count, me).wait_send())
+
+
+def sum_tables(tables, one_hot, stacks):
+    shapes = [table.shape for table in tables]
+    groups, adapters = one_hot.shape
+    count = lax.axis_size("dp") * lax.axis_size("seq")
+    tiles = -(-len(tile_places(shapes)) // count)
+    tiles += 1 - tiles % 2
+    hot = jnp.broadcast_to(one_hot[:, :, None], (groups, adapters, 128))
+    vmem = pl.BlockSpec(memory_space=pltpu.VMEM)
+    dma = pltpu.SemaphoreType.DMA
+    return pl.pallas_call(
+        partial(exchange_kernel, stacks, shapes),
+        in_specs=[vmem] * (1 + len(tables)),
+        out_specs=[vmem] * len(stacks),
+        out_shape=[
+            jax.ShapeDtypeStruct((size, adapters, *shapes[first][1:]), jnp.float32)
+            for first, size in stacks
+        ],
+        scratch_shapes=[
+            pltpu.VMEM((count, groups, tiles * 8 + adapters, 128), jnp.bfloat16),
+            pltpu.VMEM((count, groups, tiles * 8 + adapters, 128), jnp.bfloat16),
+            pltpu.VMEM((tiles * adapters * 8, 128), jnp.float32),
+            pltpu.VMEM((count, tiles * adapters * 8, 128), jnp.bfloat16),
+            dma((count,)),
+            dma((count,)),
+            dma((count,)),
+            dma((lax.axis_size("dp") // 2,)),
+            dma((count,)),
+            dma((count,)),
+            dma((count,)),
+        ],
+        compiler_params=pltpu.CompilerParams(has_side_effects=True),
+    )(hot, *tables)
 
 
 def gather_rows(rows):
@@ -141,8 +334,9 @@
     down_out,
     cotangent,
 ):
-    full_qkv = gather_rows(w_qkv)
-    full_o = gather_rows(w_o)
+    qkv_width = w_qkv.shape[1]
+    full_qkv_o = gather_rows(jnp.concatenate([w_qkv, w_o], 1))
+    full_qkv, full_o = full_qkv_o[:, :qkv_width], full_qkv_o[:, qkv_width:]
     full_up = gather_rows(w_up)
     full_down = gather_rows(w_down)
     model_width = tokens.shape[2]
@@ -191,20 +385,12 @@
     grad_normed_two, up_first, up_second = adapted_back(
         normed_two, full_up, sel_up_in, sel_up_out, reduced_up, grad_pre
     )
-    mlp_tables = (
-        fold_table(one_hot, up_first),
-        fold_table(one_hot, up_second),
-        fold_table(one_hot, down_first),
-        fold_table(one_hot, down_second),
-    )
     norm_value, norm_two_pull = jax.vjp(partial(normalize, gains=ln2_gain), after_attn)
     grad_attn = grad_layer + norm_two_pull(grad_normed_two)[0]
     grad_proj = grad_attn.astype(jnp.bfloat16)
     grad_mixed, o_first, o_second = adapted_back(
         mixed, full_o, sel_o_in, sel_o_out, reduced_o, grad_proj
     )
-    out_tables = (fold_table(one_hot, o_first), fold_table(one_hot, o_second))
-    early = lax.psum(mlp_tables + out_tables, ("dp", "seq"))
     grad_projected = attention_call(
         attend_back_kernel, keep_all, (*projected, grad_mixed.astype(jnp.bfloat16)), 3
     )
@@ -222,14 +408,20 @@
             grad_projected[column],
         )
         grad_normed = grad_normed + grad_part
-        qkv_first.append(fold_table(one_hot, first_part))
-        qkv_second.append(fold_table(one_hot, second_part))
+        qkv_first.append(first_part)
+        qkv_second.append(second_part)
     norm_one_value, norm_one_pull = jax.vjp(partial(normalize, gains=ln1_gain), tokens_f)
     grad_input = (grad_attn + norm_one_pull(grad_normed)[0]).astype(jnp.bfloat16)
-    qkv_tables = (jnp.stack(qkv_first, 0), jnp.stack(qkv_second, 0))
-    qkv_tables, early = lax.optimization_barrier((qkv_tables, early))
-    late = lax.psum(qkv_tables, ("dp", "seq"))
-    return (to_tokens(layer_out), to_tokens(grad_input), *late, *early[4:], *early[:4])
+    pieces = (
+        *qkv_first, *qkv_second, o_first, o_second, up_first, up_second, down_first, down_second
+    )
+    stacks = ((0, 3), (3, 3), (6, 1), (7, 1), (8, 1), (9, 1), (10, 1), (11, 1))
+    summed = sum_tables(pieces, one_hot, stacks)
+    results = []
+    for index, table in enumerate(summed):
+        table = table if index < 2 else table[0]
+        results.append(table if index % 2 else table.swapaxes(-1, -2))
+    return (to_tokens(layer_out), to_tokens(grad_input), *results)
 
 
 def solution(mesh):

time: 755 us -> 509 us (0.67)
  waiting for transfers between devices: 414 us -> 112 us
  Pallas kernels: 46.4 us -> 127 us
  local copies, waits for them, and re-layouts: 59.8 us -> 49.4 us
    psum x2 -> x0, waiting for transfers between devices: 240 us -> none  [the longest x1 141 us: per_device(): early = lax.psum(mlp_tables + out_tables, ('dp', 'seq'))]
    pallas_call x0 -> x1, Pallas kernels: none -> 80.4 us  [sum_tables(): pl.pallas_call(partial(exchange_kernel, stacks, shapes), in_specs=[vmem]...]
    all_gather x4 -> x3, waiting for transfers between devices: 143 us -> 95.6 us  [gather_rows(): return lax.all_gather(mine, ('dp', 'seq'), axis=0, tiled=True)]
    all_to_all x2, waiting for transfers between devices: 18.9 us -> 0.01 us  [to_tokens(): lax.all_to_all(values, 'seq', split_axis=1, concat_axis=0, tiled=True)]
    dot_general x18 -> x6, matrix products: 20.8 us -> 7.85 us  [adapted_back(): jnp.einsum('gld,glr->grd', inputs, grad_reduced, preferred_element_type=j...]
    unnamed x186 -> x158, local copies, waits for them, and re-layouts: 25 us -> 17.6 us
  transfers between devices with their start and end apart: 10 -> 7, of which waited for: 8 -> 4; matrix products, arithmetic and copies ran while one was open for 22% -> 27% of each run, Pallas kernels for 3% -> 20%
where the time goes in v3:
time: 509 us; the launch traced here: 499 us
  matrix products  135 us (27%)
  Pallas kernels  127 us (25%)
  waiting for transfers between devices  112 us (22%)
  local copies, waits for them, and re-layouts  49.4 us (10%)
  other arithmetic  39.5 us (8%)
  starting transfers between devices  20.5 us (4%)
  between operations  15.1 us (3%)
    all_gather x3, waiting for transfers between devices, gather_rows(): return lax.all_gather(mine, ('dp', 'seq'), axis=0, tiled=True)  95.6 us
    pallas_call x1, Pallas kernels, sum_tables(): pl.pallas_call(partial(exchange_kernel, stacks, shapes), in_specs=[vmem]...  80.4 us
    pallas_call x2, Pallas kernels, attention_call(): pl.pallas_call(kernel, grid=(groups, width // PAIR), in_specs=[pl.BlockSp...  46.6 us
    dot_general x6, matrix products, adapted(): jnp.einsum('gld,de->gle', inputs, weight, preferred_element_type=jnp.floa...  35.8 us
    dot_general x6, matrix products, adapted_back(): jnp.einsum('gle,de->gld', upstream, weight, preferred_element_type=jnp.fl...  33.6 us
    convert_element_type x1, other arithmetic, per_device(): activated = jax.nn.gelu(pre_act, approximate=False).astype(jnp.bfloat16)  26.1 us
    dot_general x6, matrix products, adapted_back(): jnp.einsum('glr,gdr->gld', grad_reduced, first_rank, preferred_element_ty...  20.3 us
    unnamed x158, local copies, waits for them, and re-layouts  17.6 us
  transfers between devices with their start and end apart: 7, of which 4 were waited for; matrix products, arithmetic and copies ran while one was open for 27% of the time, Pallas kernels for 20%

profile of v3, /device:TPU:31, one launch (start us, length us, event | category | flops | bytes accessed | tf_op | source)
XLA Modules:
  0.0 498.6 jit_solution(9884732679202381125)
XLA Ops:
  7.3 1.8 fusion.36
  9.9 4.3 all-to-all-start
  14.2 1.7 constant_dynamic-slice_fusion
  17.9 2.4 gather_fusion.1
  24.8 1.8 gather_fusion.2
  27.2 2.1 gather_fusion.7
  31.8 5.8 %all-to-all-start.2 = ((bf16[8,80,1024]{2,1,0:T(8,128)(2,1)}), bf16[8,80,1024]{2,1,0:T(8,128)(2,1)}, u32[]{:S(2)}, u32[]{:S(2)}) async-start(bf16[8,80,1024]{2,1,0:T(8,128)(2,1)} %param.39), calls=%async_computation.2 | async-start | bytes 2621440 | tf_op jit(solution)/shard_map/all_to_all | solution.py:310
  38.0 2.6 copy.38
  40.9 2.2 fusion.18
  44.4 16.1 %all-to-all-done.2 = bf16[8,80,1024]{2,1,0:T(8,128)(2,1)} async-done(((bf16[8,80,1024]{2,1,0:T(8,128)(2,1)}), bf16[8,80,1024]{2,1,0:T(8,128)(2,1)}, u32[]{:S(2)}, u32[]{:S(2)}) %all-to-all-start.2) | async-done | bytes 1310752 | tf_op jit(solution)/shard_map/all_to_all | solution.py:310
  60.6 1.6 copy.43
  69.1 27.3 %all-gather.4.cloned.1.call-done = bf16[1024,4096]{1,0:T(8,128)(2,1)} async-done(((bf16[32,4096]{1,0:T(8,128)(2,1)}), bf16[1024,4096]{1,0:T(8,128)(2,1)}) %all-gather.4.cloned.1.call-update) | async-done | bytes 8388624 | tf_op jit(solution)/shard_map/all_gather | solution.py:306
  96.4 3.7 fusion.27
  100.1 1.6 add_convert_fusion.5.q_ref
  103.2 1.6 add_convert_fusion.4.k_ref
  108.0 18.9 %shard_map.249 = bf16[2,320,1024]{2,1,0:T(8,128)(2,1)} custom-call(f32[2,1,320]{2,1,0:T(1,128)} %broadcast_in_dim.97.keep_ref, bf16[2,320,1024]{2,1,0:T(8,128)(2,1)} %add_convert_fusion.5.q_ref, bf16[2,320,1024]{2,1,0:T(8,128)(2,1)} %add_convert_fusion.4.k_ref, bf16[2,320,1024]{2,1,0:T(8,128)(2,1)} %add_convert_fusion.3.v_ref), custom_call_target="tpu_custom_call" | custom-call | tf_op jit(solution)/shard_map/pallas_call | solution.py:98
  126.9 1.9 convolution_convert_fusion.8
  128.8 3.6 fusion.33
  137.1 5.5 %fusion.39 = f32[2,320,4096]{2,1,0:T(8,128)} fusion(bf16[2,320,16]{1,2,0:T(8,128)(2,1)S(1)} %convolution_convert_fusion.7, bf16[2,16,4096]{2,1,0:T(8,128)(2,1)S(1)} %gather_fusion.2, pred[2]{0:T(512)(128)(4,1)S(1)} %get-tuple-element.40), kind=kOutput, calls=%fused_computation.98 | convolution fusion | flops 84017152 | bytes 10768386 | tf_op jit(solution)/shard_map/glr,gre->gle/dot_general | solution.py:27
  142.6 32.9 %all-gather.6.cloned.1.call-done = bf16[1024,4096]{1,0:T(8,128)(2,1)} async-done(((bf16[32,4096]{1,0:T(8,128)(2,1)}), bf16[1024,4096]{1,0:T(8,128)(2,1)}) %all-gather.6.cloned.1.call-update) | async-done | bytes 8388624 | tf_op jit(solution)/shard_map/all_gather | solution.py:306
  175.5 17.5 %fusion.20 = (u8[320,4096]{1,0:T(8,128)(4,1)S(1)}, u8[320,4096]{1,0:T(8,128)(4,1)S(1)}, f32[2,320,4096]{2,1,0:T(8,128)}) fusion(f32[2,320,4096]{2,1,0:T(8,128)} %fusion.39, bf16[2,320,1024]{2,1,0:T(8,128)(2,1)} %copy-done.15, bf16[1024,4096]{1,0:T(8,128)(2,1)} %all-gather.6.cloned.1.call-done), kind=kOutput, calls=%fused_computation.61 | convolution fusion | flops 5402787840 | bytes 33292288 | tf_op jit(solution)/shard_map/gld,de->gle/dot_general | solution.py:22
  193.1 26.1 %multiply_convert_fusion = (bf16[2,320,4096]{2,1,0:T(8,128)(2,1)}, f32[2,320,4096]{2,1,0:T(8,128)}) fusion(f32[2,320,4096]{2,1,0:T(8,128)} %get-tuple-element.44, u8[320,4096]{1,0:T(8,128)(4,1)S(1)} %get-tuple-element.35, u8[320,4096]{1,0:T(8,128)(4,1)S(1)} %get-tuple-element.34), kind=kLoop, calls=%fused_computation.16 | loop fusion | flops 183500800 | bytes 28835840 | tf_op jit(solution)/shard_map/convert_element_type | solution.py:372
  219.2 35.5 %all-gather.8.cloned.1.call-done = bf16[4096,1024]{1,0:T(8,128)(2,1)} async-done(((bf16[128,1024]{1,0:T(8,128)(2,1)}), bf16[4096,1024]{1,0:T(8,128)(2,1)}) %all-gather.8.cloned.1.call-update) | async-done | bytes 8388624 | tf_op jit(solution)/shard_map/all_gather | solution.py:306
  254.7 12.0 %fusion.6 = f32[2,320,4096]{2,1,0:T(8,128)} fusion(bf16[2,320,1024]{2,1,0:T(8,128)(2,1)} %copy-done.17, bf16[4096,1024]{1,0:T(8,128)(2,1)} %all-gather.8.cloned.1.call-done), kind=kOutput, calls=%fused_computation.29 | convolution fusion | flops 5368709120 | bytes 20185088 | tf_op jit(solution)/shard_map/gle,de->gld/dot_general | solution.py:40
  266.7 12.6 %add_convert_fusion = bf16[2,320,4096]{2,1,0:T(8,128)(2,1)S(1)} fusion(f32[2,320,4096]{2,1,0:T(8,128)} %get-tuple-element.39, f32[2,320,4096]{2,1,0:T(8,128)} %fusion.6, f32[2,320,4096]{2,1,0:T(8,128)} %get-tuple-element.44, bf16[2,320,16]{1,2,0:T(8,128)(2,1)S(1)} %copy-done.46, bf16[2,4096,16]{1,2,0:T(8,128)(2,1)S(1)} %gather_fusion.3, ...), kind=kOutput, calls=%fused_computation.15 | convolution fusion | flops 123338752 | bytes 36982784 | tf_op jit(solution)/shard_map/glr,gdr->gld/dot_general | solution.py:41
  282.8 8.6 %multiply_reduce_fusion.1 = (f32[2,320]{1,0:T(2,128)S(1)}, f32[2,320,1024]{2,1,0:T(8,128)S(1)}) fusion(f32[2,320,1024]{2,1,0:T(8,128)S(1)} %copy-done.6, f32[2,320]{1,0:T(2,128)S(1)} %copy-done.59, f32[1024]{0:T(1024)S(1)} %copy-done.67, f32[2,320,1024]{2,1,0:T(8,128)S(1)} %fusion.42, bf16[2,320,4096]{2,1,0:T(8,128)(2,1)S(1)} %add_convert_fusion, ...), kind=kOutput, calls=%fused_computation.50 | convolution fusion | flops 5371985408 | bytes 21505024 | tf_op jit(solution)/shard_map/gle,de->gld/dot_general | solution.py:40
  294.2 3.2 fusion.32
  297.4 1.6 add_convert_fusion.2.g_ref
  299.0 27.6 %shard_map.250 = (bf16[2,320,1024]{2,1,0:T(8,128)(2,1)}, bf16[2,320,1024]{2,1,0:T(8,128)(2,1)}, bf16[2,320,1024]{2,1,0:T(8,128)(2,1)}) custom-call(f32[2,1,320]{2,1,0:T(1,128)} %broadcast_in_dim.97.keep_ref, bf16[2,320,1024]{2,1,0:T(8,128)(2,1)} %add_convert_fusion.5.q_ref, bf16[2,320,1024]{2,1,0:T(8,128)(2,1)} %add_convert_fusion.4.k_ref, ...), custom_call_target="tpu_custom_call" | custom-call | tf_op jit(solution)/shard_map/pallas_call | solution.py:98
  326.6 1.9 convolution_convert_fusion.2
  328.5 2.0 fusion.40
  332.0 2.1 fusion.41
  337.0 4.1 convolution_convert_fusion.6
  342.8 8.0 %multiply_convert_fusion.1 = bf16[2,320,1024]{2,1,0:T(8,128)(2,1)S(1)} fusion(f32[2,320,1024]{2,1,0:T(8,128)S(1)} %copy-done.7, f32[2,320,1024]{2,1,0:T(8,128)S(1)} %fusion.43, bf16[2,320,4096]{2,1,0:T(8,128)(2,1)S(1)} %bitcast.179, bf16[4096,1024]{1,0:T(8,128)(2,1)} %all-gather.8.cloned.1.call-done, f32[2,320]{1,0:T(2,128)S(1)} %dynamic-slice_convert_fusion), kind=kOutput, calls=%fused_computation.52 | convolution fusion | flops 5371330560 | bytes 20187648 | tf_op jit(solution)/shard_map/gld,de->gle/dot_general | solution.py:22
  350.8 2.4 copy.41
  353.2 5.9 %all-to-all-start.1 = ((bf16[2,320,1024]{2,0,1:T(2,128)(2,1)}), bf16[2,320,1024]{2,0,1:T(2,128)(2,1)}, u32[]{:S(2)}, u32[]{:S(2)}) async-start(bf16[2,320,1024]{2,0,1:T(2,128)(2,1)} %copy.41), calls=%async_computation.1 | async-start | bytes 2621440 | tf_op jit(solution)/shard_map/all_to_all | solution.py:314
  359.1 1.9 convolution_convert_fusion
  360.9 2.3 fusion.62.refs_2_
  363.2 3.3 fusion.30
  366.5 3.2 fusion.28
  369.8 3.3 fusion.26
  378.8 2.4 copy.44
  385.1 4.4 all-to-all-start.3
  390.5 4.3 fusion.69.refs_9_
  394.8 1.7 fusion.70.refs_10_
  397.2 80.4 %shard_map.251 = (f32[3,8,16,1024]{3,2,1,0:T(8,128)}, f32[3,8,16,1024]{3,2,1,0:T(8,128)}, f32[1,8,16,1024]{3,2,1,0:T(8,128)}, f32[1,8,16,1024]{3,2,1,0:T(8,128)}...) custom-call(f32[2,8,128]{2,1,0:T(8,128)} %broadcast_in_dim.111.hot_r, ...), custom_call_target="tpu_custom_call" | custom-call | tf_op jit(solution)/shard_map/pallas_call | solution.py:278
  477.6 2.9 copy.42
  480.5 2.9 copy.45
  (229 shorter events, 60.2 us)
Async XLA Ops:
  7.2 89.2 %all-gather.4.cloned.1.call-start = ((), (), s32[]{:S(2)}) async-start(), calls=%async_computation.4 | async-start | bytes 8650752 | tf_op jit(solution)/shard_map/all_gather | solution.py:306
  7.2 10.0 %copy-start.69 = (s32[8]{0:T(128)S(1)}, s32[8]{0:T(128)}, u32[]{:S(2)}) copy-start(s32[8]{0:T(128)} %param.24) | copy-start | bytes 100
  7.3 10.1 %copy-start.31 = (bf16[3,8,1024,16]{2,3,1,0:T(8,128)(2,1)S(1)}, bf16[3,8,1024,16]{2,3,1,0:T(8,128)(2,1)}, u32[]{:S(2)}) copy-start(bf16[3,8,1024,16]{2,3,1,0:T(8,128)(2,1)} %param.31) | copy-start | bytes 2359300
  9.1 166.5 %all-gather.6.cloned.1.call-start = ((), (), s32[]{:S(2)}) async-start(), calls=%async_computation.5 | async-start | bytes 8650752 | tf_op jit(solution)/shard_map/all_gather | solution.py:306
  9.9 21.9 %all-to-all-start = ((bf16[8,80,1024]{2,1,0:T(8,128)(2,1)}), bf16[8,80,1024]{2,1,0:T(8,128)(2,1)S(1)}, u32[]{:S(2)}, u32[]{:S(2)}) async-start(bf16[8,80,1024]{2,1,0:T(8,128)(2,1)} %param.22), calls=%async_computation | async-start | bytes 2621440 | tf_op jit(solution)/shard_map/all_to_all | solution.py:310
  14.2 240.5 %all-gather.8.cloned.1.call-start = ((), (), s32[]{:S(2)}) async-start(), calls=%async_computation.6 | async-start | bytes 8650752 | tf_op jit(solution)/shard_map/all_gather | solution.py:306
  17.3 9.3 %copy-start.30 = (bf16[8,4096,16]{1,2,0:T(8,128)(2,1)S(1)}, bf16[8,4096,16]{1,2,0:T(8,128)(2,1)}, u32[]{:S(2)}) copy-start(bf16[8,4096,16]{1,2,0:T(8,128)(2,1)} %param.37) | copy-start | bytes 3145732
  31.8 6.2 %copy-start.22 = (bf16[8,80,1024]{2,1,0:T(8,128)(2,1)}, bf16[8,80,1024]{2,1,0:T(8,128)(2,1)S(1)}, u32[]{:S(2)}) copy-start(bf16[8,80,1024]{2,1,0:T(8,128)(2,1)S(1)} %all-to-all-done) | copy-start | bytes 3932164
  31.8 28.8 %all-to-all-start.2 = ((bf16[8,80,1024]{2,1,0:T(8,128)(2,1)}), bf16[8,80,1024]{2,1,0:T(8,128)(2,1)}, u32[]{:S(2)}, u32[]{:S(2)}) async-start(bf16[8,80,1024]{2,1,0:T(8,128)(2,1)} %param.39), calls=%async_computation.2 | async-start | bytes 2621440 | tf_op jit(solution)/shard_map/all_to_all | solution.py:310
  62.2 4.5 copy-start.8
  96.4 3.7 copy-start.54
  96.4 5.3 %copy-start.70 = (bf16[1024,4096]{1,0:T(8,128)(2,1)S(1)}, bf16[1024,4096]{1,0:T(8,128)(2,1)}, u32[]{:S(2)}) copy-start(bf16[1024,4096]{1,0:T(8,128)(2,1)} %all-gather.4.cloned.1.call-done) | copy-start | bytes 25165828
  128.8 3.6 copy-start.56
  254.7 12.0 %copy-start.46 = (bf16[2,320,16]{1,2,0:T(8,128)(2,1)S(1)}, bf16[2,320,16]{1,2,0:T(8,128)(2,1)}, u32[]{:S(2)}) copy-start(bf16[2,320,16]{1,2,0:T(8,128)(2,1)} %convolution_convert_fusion.5) | copy-start | bytes 61444
  279.2 12.2 %copy-start.11 = (bf16[2,320,4096]{2,1,0:T(8,128)(2,1)}, bf16[2,320,4096]{2,1,0:T(8,128)(2,1)S(1)}, u32[]{:S(2)}) copy-start(bf16[2,320,4096]{2,1,0:T(8,128)(2,1)S(1)} %add_convert_fusion) | copy-start | bytes 15728644
  280.7 10.7 %copy-start.48 = (bf16[2,320,16]{1,2,0:T(8,128)(2,1)}, bf16[2,320,16]{1,2,0:T(8,128)(2,1)S(1)}, u32[]{:S(2)}) copy-start(bf16[2,320,16]{1,2,0:T(8,128)(2,1)S(1)} %convolution_convert_fusion.4) | copy-start | bytes 61444
  282.8 8.7 %copy-start.63 = (f32[2,320]{1,0:T(2,128)S(1)}, f32[2,320]{1,0:T(2,128)}, u32[]{:S(2)}) copy-start(f32[2,320]{1,0:T(2,128)} %copy-done.62) | copy-start | bytes 7684
  282.8 8.7 %copy-start.61 = (f32[2,320]{1,0:T(2,128)S(1)}, f32[2,320]{1,0:T(2,128)}, u32[]{:S(2)}) copy-start(f32[2,320]{1,0:T(2,128)} %copy-done.60) | copy-start | bytes 7684
  293.7 3.7 copy-start.20
  299.0 29.5 %copy-start.35 = (bf16[3,2,1024,16]{2,3,1,0:T(8,128)(2,1)S(1)}, bf16[3,2,1024,16]{2,3,1,0:T(8,128)(2,1)}, u32[]{:S(2)}) copy-start(bf16[3,2,1024,16]{2,3,1,0:T(8,128)(2,1)} %fusion.38) | copy-start | bytes 589828
  326.6 3.9 copy-start.4
  326.6 4.9 copy-start.28
  331.5 3.5 copy-start.26
  331.5 3.5 copy-start.55
  332.0 4.0 copy-start.53
  335.0 6.6 %slice-start = ((s8[5242880]{0:T(1024)(128)(4,1)}), s8[4194304]{0:T(1024)(128)(4,1)S(1)}, s32[]{:S(2)}) async-start(s8[5242880]{0:T(1024)(128)(4,1)} %bitcast.178), calls=%async_computation.7 | async-start | bytes 8388608
  337.0 4.1 copy-start.39
  337.0 4.7 slice-start.1
  353.2 31.9 %all-to-all-start.1 = ((bf16[2,320,1024]{2,0,1:T(2,128)(2,1)}), bf16[2,320,1024]{2,0,1:T(2,128)(2,1)}, u32[]{:S(2)}, u32[]{:S(2)}) async-start(bf16[2,320,1024]{2,0,1:T(2,128)(2,1)} %copy.41), calls=%async_computation.1 | async-start | bytes 2621440 | tf_op jit(solution)/shard_map/all_to_all | solution.py:314
  359.1 4.2 copy-start.25
  363.2 3.3 copy-start.29
  369.8 3.3 copy-start.23
  369.8 3.3 copy-start.24
  369.8 3.3 copy-start.65
  377.2 4.0 copy-start.51
  378.8 3.4 copy-start.19
  378.8 4.4 copy-start.21
  378.8 4.4 copy-start.57
  383.1 6.4 %copy-start.18 = (bf16[2,320,1024]{2,1,0:T(8,128)(2,1)S(1)}, bf16[2,320,1024]{2,1,0:T(8,128)(2,1)}, u32[]{:S(2)}) copy-start(bf16[2,320,1024]{2,1,0:T(8,128)(2,1)} %copy-done.17) | copy-start | bytes 3932164
  384.1 6.4 %copy-start.41 = (bf16[2,320,16]{1,2,0:T(8,128)(2,1)S(1)}, bf16[2,320,16]{1,2,0:T(8,128)(2,1)}, u32[]{:S(2)}) copy-start(bf16[2,320,16]{1,2,0:T(8,128)(2,1)} %copy-done.40) | copy-start | bytes 61444
  385.1 9.7 %slice-start.2 = ((s8[5242880]{0:T(1024)(128)(4,1)}), s8[1048576]{0:T(1024)(128)(4,1)S(1)}, s32[]{:S(2)}) async-start(s8[5242880]{0:T(1024)(128)(4,1)} %bitcast.180), calls=%async_computation.9 | async-start | bytes 2097152
  385.1 95.4 %all-to-all-start.3 = ((bf16[2,320,1024]{2,0,1:T(2,128)(2,1)}), bf16[2,320,1024]{2,0,1:T(2,128)(2,1)}, u32[]{:S(2)}, u32[]{:S(2)}) async-start(bf16[2,320,1024]{2,0,1:T(2,128)(2,1)} %copy.44), calls=%async_computation.3 | async-start | bytes 2621440 | tf_op jit(solution)/shard_map/all_to_all | solution.py:314
  390.5 4.3 slice-start.3
  390.5 4.3 copy-start.47
  477.6 5.7 %copy-start.37 = (f32[3,8,16,1024]{3,2,1,0:T(8,128)S(1)}, f32[3,8,16,1024]{3,2,1,0:T(8,128)}, u32[]{:S(2)}) copy-start(f32[3,8,16,1024]{3,2,1,0:T(8,128)} %get-tuple-element.26) | copy-start | bytes 4718596
  480.5 4.0 copy-start.36
  484.5 3.5 copy-start.33
  488.1 3.5 copy-start.1
  (34 other events, 63.0 us)
Sparse Core Ops, SparseCore 0:
  11.4 84.9 all-gather.3
  99.8 75.6 all-gather.5
  179.0 75.6 all-gather.7

commit v4 on v3

--- a/solution.py
+++ b/solution.py
@@ -156,13 +156,6 @@
             recv_one.at[source],
             target,
         )
-
-    def loop(start, stop, body):
-        def step_body(step, carry):
-            body(step)
-            return carry
-
-        lax.fori_loop(start, stop, step_body, 0)
 
     loop(1, count, lambda step: slice_to((me + step) % count, me).start())
     received[me] = send_ref[me]
@@ -300,6 +293,166 @@
     )(hot, *tables)
 
 
+def loop(start, stop, body):
+    def step_body(step, carry):
+        body(step)
+        return carry
+
+    lax.fori_loop(start, stop, step_body, 0)
+
+
+def gather_kernel(mine_ref, full_ref, arrived, send_z, send_first, send_second, send_core, local):
+    dp, seq = lax.axis_index("dp"), lax.axis_index("seq")
+    width = lax.axis_size("seq")
+    columns = lax.axis_size("dp") // 2
+    high, low = dp // 2, dp % 2
+    seq_x = (seq + width // 2) % width
+    seq_c = seq + 1 - 2 * (seq % 2)
+    seq_xc = seq_x + 1 - 2 * (seq_x % 2)
+    halves = (0, 1)
+
+    def device(at_high, at_low, at_seq):
+        return (at_high * 2 + at_low) * width + at_seq
+
+    def remote(source_ref, target, block, half, sem):
+        return pltpu.make_async_remote_copy(
+            source_ref,
+            full_ref.at[block, half],
+            sem,
+            arrived.at[block, half],
+            device_id={"dp": target // width, "seq": target % width},
+            device_id_type=pl.DeviceIdType.MESH,
+        )
+
+    me = device(high, low, seq)
+    on_y = device(high, 1 - low, seq)
+    on_x = device(high, low, seq_x)
+    on_core = device(high, low, seq_c)
+    first = (on_y, on_x)
+    second = (on_x, on_y)
+
+    def to_z(step, half):
+        target = device((high + step) % columns, low, seq)
+        return remote(mine_ref.at[half], target, me, half, send_z.at[step, half])
+
+    def to_first(block, half):
+        source = full_ref.at[block, half]
+        return remote(source, first[half], block, half, send_first.at[block, half])
+
+    def to_second(block, half):
+        source = full_ref.at[block, half]
+        return remote(source, second[half], block, half, send_second.at[block, half])
+
+    def to_core(block, half):
+        source = full_ref.at[block, half]
+        return remote(source, on_core, block, half, send_core.at[block, half])
+
+    def column(step, at_low, at_seq):
+        return device((high + columns - step) % columns, at_low, at_seq)
+
+    keep_mine = pltpu.make_async_copy(mine_ref, full_ref.at[me], local)
+    keep_mine.start()
+
+    def start_z(step):
+        for half in halves:
+            to_z(step, half).start()
+
+    loop(1, columns, start_z)
+    keep_mine.wait()
+
+    def from_z(step):
+        block = column(step, low, seq)
+        for half in halves:
+
+            @pl.when(step > 0)
+            def _():
+                to_core(block, half).wait_recv()
+
+            to_first(block, half).start()
+            to_second(block, half).start()
+            to_core(block, half).start()
+
+    loop(0, columns, from_z)
+    by_first = ((1 - low, seq), (low, seq_x))
+    by_second = (((low, seq_x), (1 - low, seq_x)), ((1 - low, seq), (1 - low, seq_x)))
+
+    def from_first(step):
+        for half in halves:
+            block = column(step, *by_first[half])
+            to_core(block, half).wait_recv()
+            to_second(block, half).start()
+            to_core(block, half).start()
+
+    loop(0, columns, from_first)
+
+    for place in (0, 1):
+
+        def from_second(step):
+            for half in halves:
+                block = column(step, *by_second[half][place])
+                to_core(block, half).wait_recv()
+                to_core(block, half).start()
+
+        loop(0, columns, from_second)
+
+    for at_seq in (seq_c, seq_xc):
+        for at_low in (low, 1 - low):
+
+            def from_core(step):
+                for half in halves:
+                    to_core(column(step, at_low, at_seq), half).wait_recv()
+
+            loop(0, columns, from_core)
+
+    def sent_z(step):
+        for half in halves:
+            to_z(step, half).wait_send()
+
+    loop(1, columns, sent_z)
+
+    def sent_own(step):
+        for half in halves:
+            to_first(column(step, low, seq), half).wait_send()
+            to_second(column(step, low, seq), half).wait_send()
+            to_second(column(step, *by_first[half]), half).wait_send()
+
+    loop(0, columns, sent_own)
+    for at_seq in (seq, seq_x):
+        for at_low in (low, 1 - low):
+
+            def sent_core(step):
+                for half in halves:
+                    to_core(column(step, at_low, at_seq), half).wait_send()
+
+            loop(0, columns, sent_core)
+
+
+def gather_now(rows):
+    part = rows.shape[0] // lax.axis_size("seq")
+    half = rows.shape[1] // 2
+    mine = lax.dynamic_slice_in_dim(rows, lax.axis_index("seq") * part, part, 0)
+    mine = jnp.stack([mine[:, :half], mine[:, half:]])
+    count = lax.axis_size("dp") * lax.axis_size("seq")
+    vmem = pl.BlockSpec(memory_space=pltpu.VMEM)
+    dma = pltpu.SemaphoreType.DMA
+    full = pl.pallas_call(
+        gather_kernel,
+        in_specs=[vmem],
+        out_specs=vmem,
+        out_shape=jax.ShapeDtypeStruct((count, *mine.shape), mine.dtype),
+        scratch_shapes=[
+            dma((count, 2)),
+            dma((lax.axis_size("dp") // 2, 2)),
+            dma((count, 2)),
+            dma((count, 2)),
+            dma((count, 2)),
+            dma,
+        ],
+        compiler_params=pltpu.CompilerParams(has_side_effects=True),
+    )(mine)
+    return full
+
+
 def gather_rows(rows):
     part = rows.shape[0] // lax.axis_size("seq")
     mine = lax.dynamic_slice_in_dim(rows, lax.axis_index("seq") * part, part, 0)
@@ -334,9 +487,14 @@
     down_out,
     cotangent,
 ):
-    qkv_width = w_qkv.shape[1]
-    full_qkv_o = gather_rows(jnp.concatenate([w_qkv, w_o], 1))
-    full_qkv, full_o = full_qkv_o[:, :qkv_width], full_qkv_o[:, qkv_width:]
+    gathered = gather_now(jnp.concatenate([w_qkv, w_o], 1))
+    quarters = jnp.split(gathered.reshape(-1, 2, gathered.shape[2], 2, w_o.shape[1]), 2, 3)
+    quarters = [
+        quarters[place][:, half, :, 0].reshape(-1, w_o.shape[1])
+        for half in (0, 1)
+        for place in (0, 1)
+    ]
+    full_o = quarters[3]
     full_up = gather_rows(w_up)
     full_down = gather_rows(w_down)
     model_width = tokens.shape[2]
@@ -360,7 +518,7 @@
     projected = []
     reduced_qkv = []
     for column in range(3):
-        block_cols = full_qkv[:, column * model_width : (column + 1) * model_width]
+        block_cols = quarters[column]
         projection, reduced = adapted(normed, block_cols, sel_qkv_in[column], sel_qkv_out[column])
         projected.append(projection.astype(jnp.bfloat16))
         reduced_qkv.append(reduced)
@@ -398,7 +556,7 @@
     qkv_first = []
     qkv_second = []
     for column in range(3):
-        block_cols = full_qkv[:, column * model_width : (column + 1) * model_width]
+        block_cols = quarters[column]
         grad_part, first_part, second_part = adapted_back(
             normed,
             block_cols,

time: 509 us -> 528 us (1.037)
  waiting for transfers between devices: 112 us -> 14.5 us
  Pallas kernels: 127 us -> 197 us
  local copies, waits for them, and re-layouts: 49.4 us -> 99.6 us
    all_gather x3 -> x2, waiting for transfers between devices: 95.6 us -> 0.01 us  [gather_rows(): return lax.all_gather(mine, ('dp', 'seq'), axis=0, tiled=True)]
    pallas_call x0 -> x1, Pallas kernels: none -> 70.5 us  [gather_now(): pl.pallas_call(gather_kernel, in_specs=[vmem], out_specs=vmem, out_shape=...]
    slice x0 -> x1, local copies, waits for them, and re-layouts: none -> 19.2 us  [per_device(): quarters[place][:, half, :, 0].reshape(-1, w_o.shape[1])]
    unnamed x158 -> x182, local copies, waits for them, and re-layouts: 17.6 us -> 33.3 us
    reshape x0 -> x1, local copies, waits for them, and re-layouts: none -> 14.5 us  [per_device(): gathered.reshape(-1, 2, gathered.shape[2], 2, w_o.shape[1])]
  transfers between devices with their start and end apart: 7 -> 6, of which waited for: 4 -> 1; matrix products, arithmetic and copies ran while one was open for 27% -> 33% of each run, Pallas kernels for 20% -> 33%
where the time goes in v4:
time: 528 us; the launch traced here: 518 us
  Pallas kernels  197 us (37%)
  matrix products  131 us (25%)
  local copies, waits for them, and re-layouts  99.6 us (19%)
  other arithmetic  39.6 us (8%)
  starting transfers between devices  21.1 us (4%)
  between operations  15.1 us (3%)
  waiting for transfers between devices  14.5 us (3%)
    pallas_call x1, Pallas kernels, sum_tables(): pl.pallas_call(partial(exchange_kernel, stacks, shapes), in_specs=[vmem]...  80.5 us
    pallas_call x1, Pallas kernels, gather_now(): pl.pallas_call(gather_kernel, in_specs=[vmem], out_specs=vmem, out_shape=...  70.5 us
    pallas_call x2, Pallas kernels, attention_call(): pl.pallas_call(kernel, grid=(groups, width // PAIR), in_specs=[pl.BlockSp...  46.2 us
    dot_general x6, matrix products, adapted(): jnp.einsum('gld,de->gle', inputs, weight, preferred_element_type=jnp.floa...  33.8 us
    dot_general x6, matrix products, adapted_back(): jnp.einsum('gle,de->gld', upstream, weight, preferred_element_type=jnp.fl...  33.6 us
    unnamed x182, local copies, waits for them, and re-layouts  33.3 us
    convert_element_type x1, other arithmetic, per_device(): activated = jax.nn.gelu(pre_act, approximate=False).astype(jnp.bfloat16)  26.4 us
    dot_general x6, matrix products, adapted_back(): jnp.einsum('glr,gdr->gld', grad_reduced, first_rank, preferred_element_ty...  25 us
  transfers between devices with their start and end apart: 6, of which 1 were waited for; matrix products, arithmetic and copies ran while one was open for 33% of the time, Pallas kernels for 33%

profile of v4, /device:TPU:31, one launch (start us, length us, event | category | flops | bytes accessed | tf_op | source)
XLA Modules:
  0.0 517.8 jit_solution(17661196422353642494)
XLA Ops:
  9.2 4.3 all-to-all-start
  13.5 1.7 constant_dynamic-slice_fusion
  17.3 70.5 %shard_map.249 = bf16[32,2,32,2048]{3,2,1,0:T(8,128)(2,1)} custom-call(bf16[2,32,2048]{2,1,0:T(8,128)(2,1)} %pad_maximum_fusion.mine_ref), custom_call_target="tpu_custom_call" | custom-call | tf_op jit(solution)/shard_map/pallas_call | solution.py:438
  87.8 14.5 %reshape.152 = bf16[32,2,32,2,1024]{4,3,2,1,0:T(2,128)(2,1)} reshape(bf16[32,2,32,2048]{3,2,1,0:T(8,128)(2,1)} %shard_map.249) | data formatting | bytes 16777216 | tf_op jit(solution)/shard_map/reshape | solution.py:491
  102.4 19.2 %fusion.50 = (bf16[32,1,32,1,1024]{4,3,2,1,0:T(2,128)(2,1)}, bf16[32,1,32,1,1024]{4,3,2,1,0:T(2,128)(2,1)}, bf16[32,1,32,1,1024]{4,3,2,1,0:T(2,128)(2,1)}, bf16[32,1,32,1,1024]{4,3,2,1,0:T(2,128)(2,1)S(1)}) fusion(bf16[32,2,32,2,1024]{4,3,2,1,0:T(2,128)(2,1)} %reshape.152), kind=kLoop, calls=%fused_computation.134 | loop fusion | bytes 16777216 | tf_op jit(solution)/shard_map/slice | solution.py:493
  121.6 2.1 copy.54
  124.4 2.4 gather_fusion.1
  126.8 4.5 copy.55
  131.3 2.1 copy.56
  134.2 2.2 copy.57
  139.1 1.8 gather_fusion.2
  141.4 2.1 gather_fusion.7
  146.0 5.5 %all-to-all-start.2 = ((bf16[8,80,1024]{2,1,0:T(8,128)(2,1)}), bf16[8,80,1024]{2,1,0:T(8,128)(2,1)}, u32[]{:S(2)}, u32[]{:S(2)}) async-start(bf16[8,80,1024]{2,1,0:T(8,128)(2,1)} %param.39), calls=%async_computation.2 | async-start | bytes 2621440 | tf_op jit(solution)/shard_map/all_to_all | solution.py:463
  151.8 2.6 copy.42
  154.7 2.2 multiply_reduce_fusion.3
  160.1 14.5 %all-to-all-done.2 = bf16[8,80,1024]{2,1,0:T(8,128)(2,1)} async-done(((bf16[8,80,1024]{2,1,0:T(8,128)(2,1)}), bf16[8,80,1024]{2,1,0:T(8,128)(2,1)}, u32[]{:S(2)}, u32[]{:S(2)}) %all-to-all-start.2) | async-done | bytes 1310752 | tf_op jit(solution)/shard_map/all_to_all | solution.py:463
  174.6 3.1 copy.51
  183.0 1.6 add_convert_fusion.5.q_ref
  186.8 1.6 add_convert_fusion.4.k_ref
  190.1 1.6 add_convert_fusion.3.v_ref
  191.7 18.6 %shard_map.250 = bf16[2,320,1024]{2,1,0:T(8,128)(2,1)} custom-call(f32[2,1,320]{2,1,0:T(1,128)} %broadcast_in_dim.97.keep_ref, bf16[2,320,1024]{2,1,0:T(8,128)(2,1)} %add_convert_fusion.5.q_ref, bf16[2,320,1024]{2,1,0:T(8,128)(2,1)} %add_convert_fusion.4.k_ref, bf16[2,320,1024]{2,1,0:T(8,128)(2,1)} %add_convert_fusion.3.v_ref), custom_call_target="tpu_custom_call" | custom-call | tf_op jit(solution)/shard_map/pallas_call | solution.py:98
  210.3 1.8 convolution_convert_fusion.8
  212.2 3.5 fusion.55
  223.0 5.5 %fusion.29 = f32[2,320,4096]{2,1,0:T(8,128)} fusion(bf16[2,320,16]{1,2,0:T(8,128)(2,1)S(1)} %convolution_convert_fusion.7, bf16[2,16,4096]{2,1,0:T(8,128)(2,1)S(1)} %gather_fusion.2, pred[2]{0:T(512)(128)(4,1)S(1)} %get-tuple-element.40), kind=kOutput, calls=%fused_computation.89 | convolution fusion | flops 84017152 | bytes 10768386 | tf_op jit(solution)/shard_map/glr,gre->gle/dot_general | solution.py:27
  228.5 17.5 %fusion.18 = (u8[320,4096]{1,0:T(8,128)(4,1)S(1)}, u8[320,4096]{1,0:T(8,128)(4,1)S(1)}, f32[2,320,4096]{2,1,0:T(8,128)}) fusion(f32[2,320,4096]{2,1,0:T(8,128)} %fusion.29, bf16[2,320,1024]{2,1,0:T(8,128)(2,1)} %copy-done.18, bf16[1024,4096]{1,0:T(8,128)(2,1)} %all-gather.3.cloned.1.call-done), kind=kOutput, calls=%fused_computation.61 | convolution fusion | flops 5402787840 | bytes 33292288 | tf_op jit(solution)/shard_map/gld,de->gle/dot_general | solution.py:22
  246.0 26.4 %multiply_convert_fusion = (bf16[2,320,4096]{2,1,0:T(8,128)(2,1)}, f32[2,320,4096]{2,1,0:T(8,128)}) fusion(f32[2,320,4096]{2,1,0:T(8,128)} %get-tuple-element.52, u8[320,4096]{1,0:T(8,128)(4,1)S(1)} %get-tuple-element.35, u8[320,4096]{1,0:T(8,128)(4,1)S(1)} %get-tuple-element.34), kind=kLoop, calls=%fused_computation.16 | loop fusion | flops 183500800 | bytes 28835840 | tf_op jit(solution)/shard_map/convert_element_type | solution.py:530
  272.4 11.9 %fusion.6 = f32[2,320,4096]{2,1,0:T(8,128)} fusion(bf16[2,320,1024]{2,1,0:T(8,128)(2,1)} %copy-done.20, bf16[4096,1024]{1,0:T(8,128)(2,1)} %all-gather.5.cloned.1.call-done), kind=kOutput, calls=%fused_computation.29 | convolution fusion | flops 5368709120 | bytes 20185088 | tf_op jit(solution)/shard_map/gle,de->gld/dot_general | solution.py:40
  284.3 12.6 %add_convert_fusion = bf16[2,320,4096]{2,1,0:T(8,128)(2,1)S(1)} fusion(f32[2,320,4096]{2,1,0:T(8,128)} %get-tuple-element.39, f32[2,320,4096]{2,1,0:T(8,128)} %fusion.6, f32[2,320,4096]{2,1,0:T(8,128)} %get-tuple-element.52, bf16[2,320,16]{1,2,0:T(8,128)(2,1)S(1)} %copy-done.54, bf16[2,4096,16]{1,2,0:T(8,128)(2,1)S(1)} %gather_fusion.3, ...), kind=kOutput, calls=%fused_computation.15 | convolution fusion | flops 123338752 | bytes 36982784 | tf_op jit(solution)/shard_map/glr,gdr->gld/dot_general | solution.py:41
  300.4 8.9 %multiply_reduce_fusion.1 = (f32[2,320]{1,0:T(2,128)S(1)}, f32[2,320,1024]{2,1,0:T(8,128)S(1)}) fusion(f32[2,320,1024]{2,1,0:T(8,128)S(1)} %copy-done.5, f32[2,320]{1,0:T(2,128)S(1)} %broadcast_multiply_fusion.1, f32[1024]{0:T(1024)S(1)} %copy-done.78, f32[2,320,1024]{2,1,0:T(8,128)S(1)} %fusion.32, bf16[2,320,4096]{2,1,0:T(8,128)(2,1)S(1)} %add_convert_fusion, ...), kind=kOutput, calls=%fused_computation.48 | convolution fusion | flops 5371985408 | bytes 21505024 | tf_op jit(solution)/shard_map/gle,de->gld/dot_general | solution.py:40
  314.7 1.6 add_convert_fusion.2.g_ref
  316.4 27.6 %shard_map.251 = (bf16[2,320,1024]{2,1,0:T(8,128)(2,1)}, bf16[2,320,1024]{2,1,0:T(8,128)(2,1)}, bf16[2,320,1024]{2,1,0:T(8,128)(2,1)}) custom-call(f32[2,1,320]{2,1,0:T(1,128)} %broadcast_in_dim.97.keep_ref, bf16[2,320,1024]{2,1,0:T(8,128)(2,1)} %add_convert_fusion.5.q_ref, bf16[2,320,1024]{2,1,0:T(8,128)(2,1)} %add_convert_fusion.4.k_ref, ...), custom_call_target="tpu_custom_call" | custom-call | tf_op jit(solution)/shard_map/pallas_call | solution.py:98
  344.0 5.1 fusion.59
  349.6 3.1 fusion.58
  353.1 3.0 fusion.57
  356.6 2.1 fusion.30
  359.7 2.1 fusion.31
  368.0 8.1 %multiply_convert_fusion.1 = bf16[2,320,1024]{2,1,0:T(8,128)(2,1)S(1)} fusion(f32[2,320,1024]{2,1,0:T(8,128)S(1)} %copy-done.6, f32[2,320,1024]{2,1,0:T(8,128)S(1)} %fusion.33, bf16[2,320,4096]{2,1,0:T(8,128)(2,1)S(1)} %bitcast.191, bf16[4096,1024]{1,0:T(8,128)(2,1)} %all-gather.5.cloned.1.call-done, f32[2,320]{1,0:T(2,128)S(1)} %dynamic-slice_convert_fusion), kind=kOutput, calls=%fused_computation.50 | convolution fusion | flops 5371330560 | bytes 20187648 | tf_op jit(solution)/shard_map/gld,de->gle/dot_general | solution.py:22
  376.1 2.4 copy.49
  378.6 6.8 %all-to-all-start.1 = ((bf16[2,320,1024]{2,0,1:T(2,128)(2,1)}), bf16[2,320,1024]{2,0,1:T(2,128)(2,1)}, u32[]{:S(2)}, u32[]{:S(2)}) async-start(bf16[2,320,1024]{2,0,1:T(2,128)(2,1)} %copy.49), calls=%async_computation.1 | async-start | bytes 2621440 | tf_op jit(solution)/shard_map/all_to_all | solution.py:467
  385.4 2.3 fusion.62.refs_2_
  387.6 6.1 %multiply_reduce_fusion = (f32[2,320]{1,0:T(2,128)S(1)}, f32[2,320,1024]{2,1,0:T(8,128)S(1)}) fusion(f32[2,320,1024]{2,1,0:T(8,128)S(1)} %bitcast.188, f32[2,320]{1,0:T(2,128)S(1)} %div.44, f32[1024]{0:T(1024)S(1)} %copy-done.70, f32[2,320,1024]{2,1,0:T(8,128)} %fusion.59, bf16[2,320,16]{1,2,0:T(8,128)(2,1)S(1)} %convolution_convert_fusion, ...), kind=kOutput, calls=%fused_computation.44 | convolution fusion | flops 26869120 | bytes 18449920 | tf_op jit(solution)/shard_map/glr,gdr->gld/dot_general | solution.py:41
  397.8 2.4 copy.52
  404.1 4.4 all-to-all-start.3
  409.6 4.3 fusion.69.refs_9_
  413.9 1.7 fusion.70.refs_10_
  416.3 80.5 %shard_map.252 = (f32[3,8,16,1024]{3,2,1,0:T(8,128)}, f32[3,8,16,1024]{3,2,1,0:T(8,128)}, f32[1,8,16,1024]{3,2,1,0:T(8,128)}, f32[1,8,16,1024]{3,2,1,0:T(8,128)}...) custom-call(f32[2,8,128]{2,1,0:T(8,128)} %broadcast_in_dim.111.hot_r, ...), custom_call_target="tpu_custom_call" | custom-call | tf_op jit(solution)/shard_map/pallas_call | solution.py:271
  496.8 2.9 copy.50
  499.6 2.9 copy.53
  (256 shorter events, 66.4 us)
Async XLA Ops:
  7.2 9.3 %copy-start.45 = (bf16[128,3072]{1,0:T(8,128)(2,1)S(1)}, bf16[128,3072]{1,0:T(8,128)(2,1)}, u32[]{:S(2)}) copy-start(bf16[128,3072]{1,0:T(8,128)(2,1)} %param.25) | copy-start | bytes 2359300
  7.2 9.3 %copy-start.56 = (bf16[128,1024]{1,0:T(8,128)(2,1)S(1)}, bf16[128,1024]{1,0:T(8,128)(2,1)}, u32[]{:S(2)}) copy-start(bf16[128,1024]{1,0:T(8,128)(2,1)} %param.26) | copy-start | bytes 786436
  7.2 221.3 %all-gather.3.cloned.1.call-start = ((), (), s32[]{:S(2)}) async-start(), calls=%async_computation.4 | async-start | bytes 8650752 | tf_op jit(solution)/shard_map/all_gather | solution.py:459
  9.2 136.8 %all-to-all-start = ((bf16[8,80,1024]{2,1,0:T(8,128)(2,1)}), bf16[8,80,1024]{2,1,0:T(8,128)(2,1)S(1)}, u32[]{:S(2)}, u32[]{:S(2)}) async-start(bf16[8,80,1024]{2,1,0:T(8,128)(2,1)} %param.22), calls=%async_computation | async-start | bytes 2621440 | tf_op jit(solution)/shard_map/all_to_all | solution.py:463
  13.5 258.9 %all-gather.5.cloned.1.call-start = ((), (), s32[]{:S(2)}) async-start(), calls=%async_computation.5 | async-start | bytes 8650752 | tf_op jit(solution)/shard_map/all_gather | solution.py:459
  126.8 4.5 copy-start.17
  134.2 4.3 copy-start.44
  136.4 4.4 copy-start.29
  145.9 5.8 %copy-start.14 = (bf16[8,80,1024]{2,1,0:T(8,128)(2,1)}, bf16[8,80,1024]{2,1,0:T(8,128)(2,1)S(1)}, u32[]{:S(2)}) copy-start(bf16[8,80,1024]{2,1,0:T(8,128)(2,1)S(1)} %all-to-all-done) | copy-start | bytes 3932164
  146.0 28.7 %all-to-all-start.2 = ((bf16[8,80,1024]{2,1,0:T(8,128)(2,1)}), bf16[8,80,1024]{2,1,0:T(8,128)(2,1)}, u32[]{:S(2)}, u32[]{:S(2)}) async-start(bf16[8,80,1024]{2,1,0:T(8,128)(2,1)} %param.39), calls=%async_computation.2 | async-start | bytes 2621440 | tf_op jit(solution)/shard_map/all_to_all | solution.py:463
  178.9 4.1 copy-start.2
  179.4 3.6 copy-start.63
  179.8 7.0 %copy-start.61 = (bf16[2,320,16]{1,2,0:T(8,128)(2,1)}, bf16[2,320,16]{1,2,0:T(8,128)(2,1)S(1)}, u32[]{:S(2)}) copy-start(bf16[2,320,16]{1,2,0:T(8,128)(2,1)S(1)} %convolution_convert_fusion.10) | copy-start | bytes 61444
  180.3 9.8 %copy-start.59 = (bf16[2,320,16]{1,2,0:T(8,128)(2,1)}, bf16[2,320,16]{1,2,0:T(8,128)(2,1)S(1)}, u32[]{:S(2)}) copy-start(bf16[2,320,16]{1,2,0:T(8,128)(2,1)S(1)} %convolution_convert_fusion.9) | copy-start | bytes 61444
  212.2 3.6 copy-start.65
  272.4 11.9 %copy-start.54 = (bf16[2,320,16]{1,2,0:T(8,128)(2,1)S(1)}, bf16[2,320,16]{1,2,0:T(8,128)(2,1)}, u32[]{:S(2)}) copy-start(bf16[2,320,16]{1,2,0:T(8,128)(2,1)} %convolution_convert_fusion.5) | copy-start | bytes 61444
  296.8 12.4 %copy-start.10 = (bf16[2,320,4096]{2,1,0:T(8,128)(2,1)}, bf16[2,320,4096]{2,1,0:T(8,128)(2,1)S(1)}, u32[]{:S(2)}) copy-start(bf16[2,320,4096]{2,1,0:T(8,128)(2,1)S(1)} %add_convert_fusion) | copy-start | bytes 15728644
  298.3 10.9 %copy-start.57 = (bf16[2,320,16]{1,2,0:T(8,128)(2,1)}, bf16[2,320,16]{1,2,0:T(8,128)(2,1)S(1)}, u32[]{:S(2)}) copy-start(bf16[2,320,16]{1,2,0:T(8,128)(2,1)S(1)} %convolution_convert_fusion.4) | copy-start | bytes 61444
  300.4 8.9 %copy-start.74 = (f32[2,320]{1,0:T(2,128)S(1)}, f32[2,320]{1,0:T(2,128)}, u32[]{:S(2)}) copy-start(f32[2,320]{1,0:T(2,128)} %copy-done.73) | copy-start | bytes 7684
  300.4 9.0 %copy-start.72 = (f32[2,320]{1,0:T(2,128)S(1)}, f32[2,320]{1,0:T(2,128)}, u32[]{:S(2)}) copy-start(f32[2,320]{1,0:T(2,128)} %copy-done.71) | copy-start | bytes 7684
  343.9 5.2 copy-start.25
  343.9 5.6 %copy-start.27 = (bf16[2,320,1024]{2,1,0:T(8,128)(2,1)S(1)}, bf16[2,320,1024]{2,1,0:T(8,128)(2,1)}, u32[]{:S(2)}) copy-start(bf16[2,320,1024]{2,1,0:T(8,128)(2,1)} %get-tuple-element.24) | copy-start | bytes 3932164
  343.9 5.6 %copy-start.34 = (bf16[32,1,32,1,1024]{4,2,0,3,1:T(8,128)(2,1)S(1)}, bf16[32,1,32,1,1024]{4,2,0,3,1:T(8,128)(2,1)}, u32[]{:S(2)}) copy-start(bf16[32,1,32,1,1024]{4,2,0,3,1:T(8,128)(2,1)} %copy.55) | copy-start | bytes 6291460
  349.6 3.5 copy-start.28
  349.6 3.5 copy-start.32
  353.1 3.5 copy-start.40
  353.1 11.6 %slice-start = ((s8[5242880]{0:T(1024)(128)(4,1)}), s8[4194304]{0:T(1024)(128)(4,1)S(1)}, s32[]{:S(2)}) async-start(s8[5242880]{0:T(1024)(128)(4,1)} %bitcast.190), calls=%async_computation.6 | async-start | bytes 8388608
  356.6 8.1 %slice-start.1 = ((s8[5242880]{0:T(1024)(128)(4,1)}), s8[1048576]{0:T(1024)(128)(4,1)S(1)}, s32[]{:S(2)}) async-start(s8[5242880]{0:T(1024)(128)(4,1)} %bitcast.190), calls=%async_computation.7 | async-start | bytes 2097152
  358.8 4.0 copy-start.64
  359.7 4.0 copy-start.62
  378.5 9.1 %copy-start.70 = (f32[1024]{0:T(1024)S(1)}, f32[1024]{0:T(1024)}, u32[]{:S(2)}) copy-start(f32[1024]{0:T(1024)} %param.29) | copy-start | bytes 12292
  378.6 25.6 %all-to-all-start.1 = ((bf16[2,320,1024]{2,0,1:T(2,128)(2,1)}), bf16[2,320,1024]{2,0,1:T(2,128)(2,1)}, u32[]{:S(2)}, u32[]{:S(2)}) async-start(bf16[2,320,1024]{2,0,1:T(2,128)(2,1)} %copy.49), calls=%async_computation.1 | async-start | bytes 2621440 | tf_op jit(solution)/shard_map/all_to_all | solution.py:467
  387.6 6.1 %copy-start.75 = (f32[2,320]{1,0:T(2,128)S(1)}, f32[2,320]{1,0:T(2,128)}, u32[]{:S(2)}) copy-start(f32[2,320]{1,0:T(2,128)} %add.110) | copy-start | bytes 7684
  387.6 6.1 %copy-start.68 = (f32[2,320]{1,0:T(2,128)S(1)}, f32[2,320]{1,0:T(2,128)}, u32[]{:S(2)}) copy-start(f32[2,320]{1,0:T(2,128)} %rsqrt.26) | copy-start | bytes 7684
  396.3 4.0 copy-start.26
  396.3 4.0 copy-start.60
  397.8 4.4 copy-start.24
  397.8 4.4 copy-start.66
  402.2 6.4 %copy-start.21 = (bf16[2,320,1024]{2,1,0:T(8,128)(2,1)S(1)}, bf16[2,320,1024]{2,1,0:T(8,128)(2,1)}, u32[]{:S(2)}) copy-start(bf16[2,320,1024]{2,1,0:T(8,128)(2,1)} %copy-done.20) | copy-start | bytes 3932164
  403.2 6.4 %copy-start.49 = (bf16[2,320,16]{1,2,0:T(8,128)(2,1)S(1)}, bf16[2,320,16]{1,2,0:T(8,128)(2,1)}, u32[]{:S(2)}) copy-start(bf16[2,320,16]{1,2,0:T(8,128)(2,1)} %copy-done.48) | copy-start | bytes 61444
  404.1 9.8 %slice-start.2 = ((s8[5242880]{0:T(1024)(128)(4,1)}), s8[1048576]{0:T(1024)(128)(4,1)S(1)}, s32[]{:S(2)}) async-start(s8[5242880]{0:T(1024)(128)(4,1)} %bitcast.192), calls=%async_computation.8 | async-start | bytes 2097152
  404.1 95.5 %all-to-all-start.3 = ((bf16[2,320,1024]{2,0,1:T(2,128)(2,1)}), bf16[2,320,1024]{2,0,1:T(2,128)(2,1)}, u32[]{:S(2)}, u32[]{:S(2)}) async-start(bf16[2,320,1024]{2,0,1:T(2,128)(2,1)} %copy.52), calls=%async_computation.3 | async-start | bytes 2621440 | tf_op jit(solution)/shard_map/all_to_all | solution.py:467
  409.6 4.3 slice-start.3
  409.6 4.3 copy-start.55
  496.8 5.7 %copy-start.42 = (f32[3,8,16,1024]{3,2,1,0:T(8,128)S(1)}, f32[3,8,16,1024]{3,2,1,0:T(8,128)}, u32[]{:S(2)}) copy-start(f32[3,8,16,1024]{3,2,1,0:T(8,128)} %get-tuple-element.26) | copy-start | bytes 4718596
  499.6 4.0 copy-start.41
  503.7 3.5 copy-start.38
  507.2 3.5 copy-start.1
  (43 other events, 87.9 us)
Sparse Core Ops, SparseCore 0:
  11.5 95.6 all-gather.2
  110.6 79.5 all-gather.4
